TPU v7x, 128 devices: a whole 4x4x4 slice. The times are simulated.
128 devices in a mesh: rows: 16 (over z, y_hi, core), cols: 8 (over x, y_lo).
Axes of the slice: x: 4, y: 4 (y_hi: 2, y_lo: 2; y = y_hi * 2 + y_lo), z: 4, core: 2. Of those that a mesh axis runs over, the one named last changes fastest.
Arguments:
- feat_query: bfloat16 [256, 512, 2048], P('rows', 'cols'), may hold values from -30 to 30
- feat_key: bfloat16 [256, 512, 2048], P('rows', 'cols'), may hold values from -30 to 30
- w_hidden: bfloat16 [2048, 2048], replicated, may hold values from -0.125 to 0.125
- w_out: bfloat16 [2048, 256], replicated, may hold values from -0.125 to 0.125
- w_prop: bfloat16 [256, 256], replicated, may hold values from -0.375 to 0.375
- valid_mask: int32 [256, 512], P('rows', 'cols'), may hold values 0 or 1
- neg_shard: int32 [16, 8, 8, 2], P('rows', 'cols'), may hold values from 0 to 15, as said below
- neg_block: int32 [16, 8, 8, 2], P('rows', 'cols'), may hold values from 0 to 7
Outputs:
- loss_map: float32 [256, 512], P('rows', 'cols')
Inputs may be any that keep to these rules, and one draw needn't show every extreme that they name: `neg_shard`: among the 16 entries of one tile, no shard number appears more than 2 times, and some shard number appears exactly 2 times.
All inputs are finite; a program needn't handle non-finite values. No bound on the sum of `valid_mask` on one device may be relied on, other than what follows from the above.
Results may differ from a plain program's by a relative error of at most 0.0006.
Values may be sent and summed in bfloat16 or wider, within the bound.
No kernel may reach another device: no remote copies, remote signals or barrier semaphores. Data moves between devices by JAX's collectives and lax.ppermute only.
A program may use at most 128 MiB of HBM per device.

v0:
```python
import jax
import jax.numpy as jnp
from jax import lax
from jax.sharding import PartitionSpec as P

epsilon = 1e-06
sharpness_divisor = 0.1


def from_partner(value, axis, bit):
    mask = 2**bit
    pairs = [(source, source ^ mask) for source in range(lax.axis_size(axis))]
    return lax.ppermute(value, axis, pairs)


def padded_2(array, sides, width):
    for axis, dim in sides:
        devices, length = (lax.axis_size(axis), array.shape[dim])
        up = [(i, (i + 1) % devices) for i in range(devices - 1)]
        down = [(j, i) for i, j in up]
        last = lax.slice_in_dim(array, length - width, length, axis=dim)
        leading = lax.slice_in_dim(array, 0, width, axis=dim)
        before = lax.ppermute(last, axis, up)
        after = lax.ppermute(leading, axis, down)
        array = jnp.concatenate([before, array, after], axis=dim)
    return array


def normalize(vector):
    return vector * lax.rsqrt(jnp.sum(vector * vector, axis=-1, keepdims=True) + epsilon)


def project(feat_map, w_hidden, w_out):
    height, columns, channels = feat_map.shape
    flat_rows = feat_map.reshape(height * columns, channels)
    hidden = jnp.maximum(
        jnp.dot(flat_rows, w_hidden, preferred_element_type=jnp.float32), 0.0
    ).astype(jnp.bfloat16)
    embedded = normalize(jnp.dot(hidden, w_out, preferred_element_type=jnp.float32)).astype(
        jnp.bfloat16
    )
    return embedded.reshape(height, columns, -1)


def per_device(feat_query, feat_key, w_hidden, w_out, w_prop, valid_mask, neg_shard, neg_block):
    height, columns, channels = feat_query.shape
    per_tile = height * columns // 128
    target_embedding_lattice = project(feat_key, w_hidden, w_out)
    proj_width = target_embedding_lattice.shape[-1]
    key_blocks = target_embedding_lattice.reshape(per_tile, 128, proj_width)
    bit_total = lax.axis_size("cols").bit_length() - 1
    bit_order = list(range(bit_total))
    current = target_embedding_lattice
    for bit_number in bit_order:
        current = from_partner(current, "cols", bit_number)
    partner = current[:, ::-1]
    shard_ids = neg_shard.reshape(-1)
    block_ids = neg_block.reshape(-1)
    gathered_keys = lax.all_gather(key_blocks, "rows", axis=0, tiled=True)
    contrast_pair_agreements = gathered_keys[shard_ids * per_tile + block_ids]
    contrast_pair_agreements = contrast_pair_agreements.reshape(per_tile, -1, 128, proj_width)
    query_map = project(feat_query, w_hidden, w_out)
    padded = padded_2(query_map, (("rows", 0), ("cols", 1)), 1)
    carried = jnp.dot(padded.reshape(-1, proj_width), w_prop, preferred_element_type=jnp.float32)
    carried = carried.reshape(height + 2, columns + 2, proj_width)
    spread = jnp.zeros((height, columns, proj_width), jnp.float32)
    for row_off in range(3):
        for col_off in range(3):
            beside = padded[row_off : row_off + height, col_off : col_off + columns]
            cosine = jnp.einsum(
                "hwp,hwp->hw", query_map, beside, preferred_element_type=jnp.float32
            )
            weight = jnp.maximum(cosine, 0.0) ** 2
            spread = (
                spread
                + weight[..., None]
                * carried[row_off : row_off + height, col_off : col_off + columns]
            )
    diffused_pixel_embeddings = normalize(spread).astype(jnp.bfloat16)
    matched_pair_agreement = (
        jnp.einsum(
            "hwp,hwp->hw", diffused_pixel_embeddings, partner, preferred_element_type=jnp.float32
        )
        / sharpness_divisor
    )
    query_blocks = diffused_pixel_embeddings.reshape(per_tile, 128, proj_width)
    cosine_match_energies = (
        jnp.einsum(
            "bip,bnjp->binj",
            query_blocks,
            contrast_pair_agreements,
            preferred_element_type=jnp.float32,
        )
        / sharpness_divisor
    )
    negsum = jnp.sum(jnp.exp(cosine_match_energies), axis=(2, 3)).reshape(height, columns)
    denominator = jnp.exp(matched_pair_agreement) + negsum
    return valid_mask.astype(jnp.float32) * (jnp.log(denominator) - matched_pair_agreement)


def solution(mesh):
    in_specs = (
        P("rows", "cols", None),
        P("rows", "cols", None),
        P(),
        P(),
        P(),
        P("rows", "cols"),
        P("rows", "cols", None, None),
        P("rows", "cols", None, None),
    )
    out_specs = P("rows", "cols")
    return jax.shard_map(
        per_device, mesh=mesh, in_specs=in_specs, out_specs=out_specs, check_vma=False
    )
```

profile of v0, /device:TPU:1, one launch (start us, length us, event | category | flops | bytes accessed | tf_op | source)
XLA Modules:
  0.0 112.2 jit_solution(3543612557265567665)
XLA Ops:
  6.5 1.2 %copy-done = bf16[2048,256]{1,0:T(8,128)(2,1)S(1)} copy-done((bf16[2048,256]{1,0:T(8,128)(2,1)S(1)}, bf16[2048,256]{1,0:T(8,128)(2,1)}, u32[]{:S(2)}) %copy-start) | copy-done | bytes 1048600
  7.8 14.8 %multiply_reduce_fusion = (f32[1024]{0:T(1024)S(1)}, f32[1024,256]{1,0:T(8,128)S(1)}) fusion(bf16[2048,256]{1,0:T(8,128)(2,1)S(1)} %copy-done, bf16[1024,2048]{1,0:T(8,128)(2,1)} %bitcast.38, bf16[2048,2048]{1,0:T(8,128)(2,1)} %param.10), kind=kOutput, calls=%fused_computation.46 | convolution fusion | flops 9668393984 | bytes 14684160 | tf_op jit(solution)/shard_map/dot_general | solution.py:39
  22.5 1.1 multiply_convert_fusion
  23.6 0.0 all-gather.2.cloned.1.call-update
  23.6 15.0 %multiply_reduce_fusion.2 = (f32[1024]{0:T(1024)S(1)}, f32[1024,256]{1,0:T(8,128)S(1)}) fusion(bf16[2048,256]{1,0:T(8,128)(2,1)S(1)} %copy-done, bf16[1024,2048]{1,0:T(8,128)(2,1)} %bitcast.39, bf16[2048,2048]{1,0:T(8,128)(2,1)} %param.10), kind=kOutput, calls=%fused_computation.50 | convolution fusion | flops 9668393984 | bytes 14684160 | tf_op jit(solution)/shard_map/dot_general | solution.py:39
  38.6 0.0 copy-start.5
  38.6 0.2 multiply_convert_fusion.2
  38.9 6.2 %collective-permute-start = (bf16[1,64,256]{2,1,0:T(8,128)(2,1)S(1)}, bf16[1,64,256]{2,1,0:T(8,128)(2,1)S(1)}, u32[]{:S(2)}, u32[]{:S(2)}) collective-permute-start(bf16[1,64,256]{2,1,0:T(8,128)(2,1)S(1)} %get-tuple-element.25), channel_id=1, source_target_pairs={{0,8},{8,16},{16,24},{24,32},{32,40},{40,48},{48,56},{56,64},{64,7... | collective-permute-start | bytes 98312 | tf_op jit(solution)/shard_map/ppermute | solution.py:23
  45.1 1.9 %collective-permute-start.1 = (bf16[1,64,256]{2,1,0:T(8,128)(2,1)S(1)}, bf16[1,64,256]{2,1,0:T(8,128)(2,1)S(1)}, u32[]{:S(2)}, u32[]{:S(2)}) collective-permute-start(bf16[1,64,256]{2,1,0:T(8,128)(2,1)S(1)} %get-tuple-element.26), channel_id=1, source_target_pairs={{8,0},{16,8},{24,16},{32,24},{40,32},{48,40},{56,48},{64,56},{72,6... | collective-permute-start | bytes 98312 | tf_op jit(solution)/shard_map/ppermute | solution.py:24
  47.0 0.5 collective-permute-start.4
  47.5 0.1 copy.11
  47.6 0.1 add.90
  47.7 4.5 %collective-permute-done.1 = bf16[1,64,256]{2,1,0:T(8,128)(2,1)S(1)} collective-permute-done((bf16[1,64,256]{2,1,0:T(8,128)(2,1)S(1)}, bf16[1,64,256]{2,1,0:T(8,128)(2,1)S(1)}, u32[]{:S(2)}, u32[]{:S(2)}) %collective-permute-start.1) | collective-permute-done | bytes 32800 | tf_op jit(solution)/shard_map/ppermute | solution.py:24
  52.3 2.6 %collective-permute-start.2 = (bf16[18,1,256]{2,1,0:T(2,128)(2,1)S(1)}, bf16[18,1,256]{2,1,0:T(2,128)(2,1)S(1)}, u32[]{:S(2)}, u32[]{:S(2)}) collective-permute-start(bf16[18,1,256]{2,1,0:T(2,128)(2,1)S(1)} %get-tuple-element.23), channel_id=1, source_target_pairs={{0,1},{1,2},{2,3},{3,4},{4,5},{5,6},{6,7},{8,9},{9,10},{10,11},{11... | collective-permute-start | bytes 27656 | tf_op jit(solution)/shard_map/ppermute | solution.py:23
  54.9 1.3 %collective-permute-start.3 = (bf16[18,1,256]{2,1,0:T(2,128)(2,1)S(1)}, bf16[18,1,256]{2,1,0:T(2,128)(2,1)S(1)}, u32[]{:S(2)}, u32[]{:S(2)}) collective-permute-start(bf16[18,1,256]{2,1,0:T(2,128)(2,1)S(1)} %get-tuple-element.24), channel_id=1, source_target_pairs={{1,0},{2,1},{3,2},{4,3},{5,4},{6,5},{7,6},{9,8},{10,9},{11,10},{12... | collective-permute-start | bytes 27656 | tf_op jit(solution)/shard_map/ppermute | solution.py:24
  56.2 1.5 %collective-permute-done.2 = bf16[18,1,256]{2,1,0:T(2,128)(2,1)S(1)} collective-permute-done((bf16[18,1,256]{2,1,0:T(2,128)(2,1)S(1)}, bf16[18,1,256]{2,1,0:T(2,128)(2,1)S(1)}, u32[]{:S(2)}, u32[]{:S(2)}) %collective-permute-start.2) | collective-permute-done | bytes 9248 | tf_op jit(solution)/shard_map/ppermute | solution.py:23
  57.7 1.9 %collective-permute-done.3 = bf16[18,1,256]{2,1,0:T(2,128)(2,1)S(1)} collective-permute-done((bf16[18,1,256]{2,1,0:T(2,128)(2,1)S(1)}, bf16[18,1,256]{2,1,0:T(2,128)(2,1)S(1)}, u32[]{:S(2)}, u32[]{:S(2)}) %collective-permute-start.3) | collective-permute-done | bytes 9248 | tf_op jit(solution)/shard_map/ppermute | solution.py:24
  59.6 0.4 pad_maximum_fusion
  60.0 1.5 %fusion.4 = (f32[16,64]{1,0:T(8,128)S(1)}, f32[16,64]{1,0:T(8,128)S(1)}, f32[16,64]{1,0:T(8,128)S(1)}, f32[16,64]{1,0:T(8,128)S(1)}, f32[16,64]{1,0:T(8,128)S(1)...) fusion(bf16[16,64,256]{2,1,0:T(8,128)(2,1)S(1)} %bitcast.32, ...), kind=kLoop, calls=%fused_computation.17 | loop fusion | flops 7592960 | bytes 3772416 | tf_op jit(solution)/shard_map/hwp,hwp->hw/dot_general | solution.py:70
  61.6 1.3 %collective-permute-start.5 = (bf16[16,64,256]{2,1,0:T(8,128)(2,1)S(1)}, bf16[16,64,256]{2,1,0:T(8,128)(2,1)S(1)}, u32[]{:S(2)}, u32[]{:S(2)}) collective-permute-start(bf16[16,64,256]{2,1,0:T(8,128)(2,1)S(1)} %collective-permute-done.4), channel_id=1, source_target_pairs={{0,2},{1,3},{2,0},{3,1},{4,6},{5,7},{6,4},{7,5},{8,10},{9,11},{10,... | collective-permute-start | bytes 1572872 | tf_op jit(solution)/shard_map/ppermute | solution.py:13
  62.9 0.4 fusion.22
  63.3 10.2 %collective-permute-done.5 = bf16[16,64,256]{2,1,0:T(8,128)(2,1)S(1)} collective-permute-done((bf16[16,64,256]{2,1,0:T(8,128)(2,1)S(1)}, bf16[16,64,256]{2,1,0:T(8,128)(2,1)S(1)}, u32[]{:S(2)}, u32[]{:S(2)}) %collective-permute-start.5) | collective-permute-done | bytes 524320 | tf_op jit(solution)/shard_map/ppermute | solution.py:13
  73.5 2.5 %collective-permute-start.6 = (bf16[16,64,256]{2,1,0:T(8,128)(2,1)S(1)}, bf16[16,64,256]{2,1,0:T(8,128)(2,1)S(1)}, u32[]{:S(2)}, u32[]{:S(2)}) collective-permute-start(bf16[16,64,256]{2,1,0:T(8,128)(2,1)S(1)} %collective-permute-done.5), channel_id=1, source_target_pairs={{0,4},{1,5},{2,6},{3,7},{4,0},{5,1},{6,2},{7,3},{8,12},{9,13},{10,... | collective-permute-start | bytes 1572872 | tf_op jit(solution)/shard_map/ppermute | solution.py:13
  76.0 1.9 %multiply_reduce_fusion.1 = (f32[16,64]{1,0:T(8,128)S(1)}, f32[16,64,256]{2,1,0:T(8,128)S(1)}) fusion(f32[18,66,256]{2,1,0:T(8,128)S(1)} %fusion.22, f32[16,64]{1,0:T(8,128)S(1)} %get-tuple-element.31, f32[16,64]{1,0:T(8,128)S(1)} %get-tuple-element.32, f32[16,64]{1,0:T(8,128)S(1)} %get-tuple-element.33, f32[16,64]{1,0:T(8,128)S(1)} %get-tuple-element.34, ...), kind=kLoop, calls=%fused_computation.48 | loop fusion | flops 4979712 | bytes 10526720 | tf_op jit(solution)/shard_map/reduce_sum | solution.py:30
  77.9 9.7 %collective-permute-done.6 = bf16[16,64,256]{2,1,0:T(8,128)(2,1)S(1)} collective-permute-done((bf16[16,64,256]{2,1,0:T(8,128)(2,1)S(1)}, bf16[16,64,256]{2,1,0:T(8,128)(2,1)S(1)}, u32[]{:S(2)}, u32[]{:S(2)}) %collective-permute-start.6) | collective-permute-done | bytes 524320 | tf_op jit(solution)/shard_map/ppermute | solution.py:13
  87.6 0.4 rev.3
  87.9 0.4 fusion.21
  88.3 11.9 %all-gather.2.cloned.1.call-done = bf16[128,128,256]{2,1,0:T(8,128)(2,1)} async-done(((bf16[8,128,256]{2,1,0:T(8,128)(2,1)}), bf16[128,128,256]{2,1,0:T(8,128)(2,1)}) %all-gather.2.cloned.1.call-update) | async-done | bytes 8388624 | tf_op jit(solution)/shard_map/all_gather | solution.py:59
  100.2 4.0 %gather_fusion = bf16[16,128,256]{2,1,0:T(8,128)(2,1)S(1)} fusion(bf16[128,128,256]{2,1,0:T(8,128)(2,1)} %all-gather.2.cloned.1.call-done, s32[1024]{0:T(1024)S(1)} %pad_clamp_fusion), kind=kCustom, calls=%fused_computation | custom fusion | bytes 2097216 | tf_op jit(solution)/shard_map/gather | solution.py:60
  104.2 0.4 fusion.1
  104.7 0.1 reshape.94
  104.8 0.6 subtract_multiply_fusion
  (26 shorter events, 0.1 us)
Async XLA Ops:
  6.5 1.2 %copy-start = (bf16[2048,256]{1,0:T(8,128)(2,1)S(1)}, bf16[2048,256]{1,0:T(8,128)(2,1)}, u32[]{:S(2)}) copy-start(bf16[2048,256]{1,0:T(8,128)(2,1)} %param.11) | copy-start | bytes 3145732
  6.5 93.7 %all-gather.2.cloned.1.call-start = ((), (), s32[]{:S(2)}) async-start(), calls=%async_computation | async-start | bytes 8912896 | tf_op jit(solution)/shard_map/all_gather | solution.py:59
  23.6 23.4 %copy-start.1 = (bf16[1024,256]{1,0:T(8,128)(2,1)S(1)}, bf16[1024,256]{1,0:T(8,128)(2,1)}, u32[]{:S(2)}) copy-start(bf16[1024,256]{1,0:T(8,128)(2,1)} %multiply_convert_fusion) | copy-start | bytes 1572868
  23.6 23.9 %copy-start.3 = (s32[1,1,8,2]{2,3,1,0:T(2,128)S(1)}, s32[1,1,8,2]{2,3,1,0:T(2,128)}, u32[]{:S(2)}) copy-start(s32[1,1,8,2]{2,3,1,0:T(2,128)} %param.15) | copy-start | bytes 196
  23.6 23.9 %copy-start.4 = (s32[1,1,8,2]{2,3,1,0:T(2,128)S(1)}, s32[1,1,8,2]{2,3,1,0:T(2,128)}, u32[]{:S(2)}) copy-start(s32[1,1,8,2]{2,3,1,0:T(2,128)} %param.14) | copy-start | bytes 196
  38.6 24.3 %copy-start.5 = (bf16[256,256]{1,0:T(8,128)(2,1)S(1)}, bf16[256,256]{1,0:T(8,128)(2,1)}, u32[]{:S(2)}) copy-start(bf16[256,256]{1,0:T(8,128)(2,1)} %param.12) | copy-start | bytes 393220
  38.9 8.8 %collective-permute-start = (bf16[1,64,256]{2,1,0:T(8,128)(2,1)S(1)}, bf16[1,64,256]{2,1,0:T(8,128)(2,1)S(1)}, u32[]{:S(2)}, u32[]{:S(2)}) collective-permute-start(bf16[1,64,256]{2,1,0:T(8,128)(2,1)S(1)} %get-tuple-element.25), channel_id=1, source_target_pairs={{0,8},{8,16},{16,24},{24,32},{32,40},{40,48},{48,56},{56,64},{64,7... | collective-permute-start | bytes 98312 | tf_op jit(solution)/shard_map/ppermute | solution.py:23
  45.1 7.1 %collective-permute-start.1 = (bf16[1,64,256]{2,1,0:T(8,128)(2,1)S(1)}, bf16[1,64,256]{2,1,0:T(8,128)(2,1)S(1)}, u32[]{:S(2)}, u32[]{:S(2)}) collective-permute-start(bf16[1,64,256]{2,1,0:T(8,128)(2,1)S(1)} %get-tuple-element.26), channel_id=1, source_target_pairs={{8,0},{16,8},{24,16},{32,24},{40,32},{48,40},{56,48},{64,56},{72,6... | collective-permute-start | bytes 98312 | tf_op jit(solution)/shard_map/ppermute | solution.py:24
  47.0 14.6 %collective-permute-start.4 = (bf16[16,64,256]{2,1,0:T(8,128)(2,1)S(1)}, bf16[16,64,256]{2,1,0:T(8,128)(2,1)S(1)}, u32[]{:S(2)}, u32[]{:S(2)}) collective-permute-start(bf16[16,64,256]{2,1,0:T(8,128)(2,1)S(1)} %bitcast.35), channel_id=1, source_target_pairs={{0,1},{1,0},{2,3},{3,2},{4,5},{5,4},{6,7},{7,6},{8,9},{9,8},{10,11... | collective-permute-start | bytes 1572872 | tf_op jit(solution)/shard_map/ppermute | solution.py:13
  52.3 5.5 %collective-permute-start.2 = (bf16[18,1,256]{2,1,0:T(2,128)(2,1)S(1)}, bf16[18,1,256]{2,1,0:T(2,128)(2,1)S(1)}, u32[]{:S(2)}, u32[]{:S(2)}) collective-permute-start(bf16[18,1,256]{2,1,0:T(2,128)(2,1)S(1)} %get-tuple-element.23), channel_id=1, source_target_pairs={{0,1},{1,2},{2,3},{3,4},{4,5},{5,6},{6,7},{8,9},{9,10},{10,11},{11... | collective-permute-start | bytes 27656 | tf_op jit(solution)/shard_map/ppermute | solution.py:23
  54.9 4.7 %collective-permute-start.3 = (bf16[18,1,256]{2,1,0:T(2,128)(2,1)S(1)}, bf16[18,1,256]{2,1,0:T(2,128)(2,1)S(1)}, u32[]{:S(2)}, u32[]{:S(2)}) collective-permute-start(bf16[18,1,256]{2,1,0:T(2,128)(2,1)S(1)} %get-tuple-element.24), channel_id=1, source_target_pairs={{1,0},{2,1},{3,2},{4,3},{5,4},{6,5},{7,6},{9,8},{10,9},{11,10},{12... | collective-permute-start | bytes 27656 | tf_op jit(solution)/shard_map/ppermute | solution.py:24
  61.6 11.9 %collective-permute-start.5 = (bf16[16,64,256]{2,1,0:T(8,128)(2,1)S(1)}, bf16[16,64,256]{2,1,0:T(8,128)(2,1)S(1)}, u32[]{:S(2)}, u32[]{:S(2)}) collective-permute-start(bf16[16,64,256]{2,1,0:T(8,128)(2,1)S(1)} %collective-permute-done.4), channel_id=1, source_target_pairs={{0,2},{1,3},{2,0},{3,1},{4,6},{5,7},{6,4},{7,5},{8,10},{9,11},{10,... | collective-permute-start | bytes 1572872 | tf_op jit(solution)/shard_map/ppermute | solution.py:13
  73.5 14.1 %collective-permute-start.6 = (bf16[16,64,256]{2,1,0:T(8,128)(2,1)S(1)}, bf16[16,64,256]{2,1,0:T(8,128)(2,1)S(1)}, u32[]{:S(2)}, u32[]{:S(2)}) collective-permute-start(bf16[16,64,256]{2,1,0:T(8,128)(2,1)S(1)} %collective-permute-done.5), channel_id=1, source_target_pairs={{0,4},{1,5},{2,6},{3,7},{4,0},{5,1},{6,2},{7,3},{8,12},{9,13},{10,... | collective-permute-start | bytes 1572872 | tf_op jit(solution)/shard_map/ppermute | solution.py:13
  77.9 26.9 %copy-start.2 = (s32[16,64]{1,0:T(8,128)S(1)}, s32[16,64]{1,0:T(8,128)}, u32[]{:S(2)}) copy-start(s32[16,64]{1,0:T(8,128)} %param.13) | copy-start | bytes 12292
Sparse Core Ops, SparseCore 0:
  23.7 76.4 all-gather.1
where the time goes:
time: 112 us
  waiting for transfers between devices  39.7 us (35%)
  matrix products  30.5 us (27%)
  starting transfers between devices  16.3 us (15%)
  between operations  13.6 us (12%)
  other arithmetic  6.16 us (6%)
  local copies, waits for them, and re-layouts  5.84 us (5%)
    dot_general x2, matrix products, project(): jnp.dot(hidden, w_out, preferred_element_type=jnp.float32)  29.7 us
    ppermute x3, waiting for transfers between devices, from_partner(): return lax.ppermute(value, axis, pairs)  19.9 us
    all_gather x1, waiting for transfers between devices, per_device(): gathered_keys = lax.all_gather(key_blocks, 'rows', axis=0, tiled=True)  11.9 us
    ppermute x2, starting transfers between devices, padded_2(): before = lax.ppermute(last, axis, up)  8.85 us
    ppermute x2, waiting for transfers between devices, padded_2(): after = lax.ppermute(leading, axis, down)  6.42 us
    ppermute x3, starting transfers between devices, from_partner(): return lax.ppermute(value, axis, pairs)  4.26 us
    gather x1, local copies, waits for them, and re-layouts, per_device(): contrast_pair_agreements = gathered_keys[shard_ids * per_tile + block_ids]  3.99 us
    ppermute x2, starting transfers between devices, padded_2(): after = lax.ppermute(leading, axis, down)  3.21 us
  transfers between devices with their start and end apart: 8, of which 6 were waited for; matrix products, arithmetic and copies ran while one was open for 18% of the time, Pallas kernels for 0%

commit v1 on v0

v1 whole, which is shorter than its diff:
```python
import functools

import jax
import jax.numpy as jnp
from jax import lax
from jax.experimental import pallas as pl
from jax.experimental.pallas import tpu as pltpu
from jax.sharding import PartitionSpec as P


epsilon = 1e-06
inverse_divisor = 10.0
CAP = 2
LANES = 128
VMEM = pl.BlockSpec(memory_space=pltpu.VMEM)
SMEM = pl.BlockSpec(memory_space=pltpu.SMEM)
ANY = pl.BlockSpec(memory_space=pl.ANY)
LIMIT = 60 * 2**20
SMALL = pltpu.CompilerParams(vmem_limit_bytes=12 * 2**20)
f32 = jnp.float32
bf16 = jnp.bfloat16


def normalize(vector):
    return vector * lax.rsqrt(jnp.sum(vector * vector, axis=-1, keepdims=True) + epsilon)


def transposed_dot(left, right):
    return lax.dot_general(left, right, (((1,), (1,)), ((), ())), preferred_element_type=f32)


def plan_kernel(shard_ref, block_ref, want_ref, slot_ref):
    _, _, per, blocks = shard_ref.shape
    shards = want_ref.shape[0]
    rows = lax.broadcasted_iota(jnp.int32, (shards, LANES), 0)
    lanes = lax.broadcasted_iota(jnp.int32, (shards, LANES), 1)
    want = jnp.zeros((shards, LANES), jnp.int32)
    chosen = []
    for block in range(blocks):
        for n in range(per):
            shard = shard_ref[0, 0, n, block]
            rank = jnp.int32(0)
            for other in chosen:
                rank = rank + (other == shard).astype(jnp.int32)
            rank = jnp.minimum(rank, CAP - 1)
            chosen.append(shard)
            slot_ref[block * per + n] = shard * CAP + rank
            want = jnp.where((rows == shard) & (lanes == rank), block_ref[0, 0, n, block], want)
    want_ref[...] = want.reshape(want_ref.shape)


def plan_slots(neg_shard, neg_block, shards):
    entries = neg_shard.size
    return pl.pallas_call(
        plan_kernel,
        in_specs=[SMEM, SMEM],
        out_specs=[VMEM, SMEM],
        out_shape=[
            jax.ShapeDtypeStruct((shards, 1, LANES), jnp.int32),
            jax.ShapeDtypeStruct((entries,), jnp.int32),
        ],
        compiler_params=SMALL,
        name="plan_slots",
    )(neg_shard.transpose(0, 1, 3, 2), neg_block.transpose(0, 1, 3, 2))


ROWS = 256
PARTS = 8


def project_kernel(feat_ref, hidden_hbm, out_hbm, map_ref, hidden_w, out_w, sem):
    step = pl.program_id(0)
    span = hidden_w.shape[1] // PARTS

    def piece(index):
        cut = pl.ds(index * span, span)
        return pltpu.make_async_copy(hidden_hbm.at[:, cut], hidden_w.at[:, cut], sem.at[index])

    def tail():
        return pltpu.make_async_copy(out_hbm, out_w, sem.at[PARTS])

    def finish(raw):
        map_ref[...] = normalize(raw).astype(map_ref.dtype)

    def layer(cut):
        hidden = jnp.dot(feat_ref[...], hidden_w[:, cut], preferred_element_type=f32)
        hidden = jnp.maximum(hidden, 0.0).astype(bf16)
        return jnp.dot(hidden, out_w[cut, :], preferred_element_type=f32)

    @pl.when(step == 0)
    def _():
        piece(0).start()
        piece(1).start()
        tail().start()
        total = None
        for index in range(0, PARTS, 2):
            piece(index).wait()
            piece(index + 1).wait()
            if index == 0:
                tail().wait()
            if index + 2 < PARTS:
                piece(index + 2).start()
                piece(index + 3).start()
            term = layer(pl.ds(index * span, 2 * span))
            total = term if total is None else total + term
        finish(total)

    @pl.when(step > 0)
    def _():
        finish(layer(pl.ds(0, hidden_w.shape[1])))


def project(feat_map, w_hidden, w_out):
    height, columns, channels = feat_map.shape
    pixels = height * columns
    hidden, width = w_out.shape
    return pl.pallas_call(
        project_kernel,
        grid=(pixels // ROWS,),
        in_specs=[pl.BlockSpec((ROWS, channels), lambda i: (i, 0)), ANY, ANY],
        out_specs=pl.BlockSpec((ROWS, width), lambda i: (i, 0)),
        out_shape=jax.ShapeDtypeStruct((pixels, width), bf16),
        scratch_shapes=[
            pltpu.VMEM((channels, hidden), bf16),
            pltpu.VMEM((hidden, width), bf16),
            pltpu.SemaphoreType.DMA((PARTS + 1,)),
        ],
        compiler_params=pltpu.CompilerParams(vmem_limit_bytes=LIMIT),
        cost_estimate=pl.CostEstimate(
            flops=2 * pixels * hidden * (channels + width),
            bytes_accessed=2 * (pixels * channels + hidden * (channels + width)),
            transcendentals=0,
        ),
    )(feat_map.reshape(pixels, channels), w_hidden, w_out)


def pack_kernel(req_ref, keys_ref, out_ref, sem):
    for shard in range(out_ref.shape[0]):
        for rank in range(CAP):
            source = keys_ref.at[req_ref[shard, 0, rank]]
            pltpu.make_async_copy(source, out_ref.at[shard, rank], sem).start()
    pltpu.make_async_copy(out_ref, out_ref, sem).wait()


def pack(req, key_blocks):
    return pl.pallas_call(
        pack_kernel,
        in_specs=[SMEM, VMEM],
        out_specs=ANY,
        out_shape=jax.ShapeDtypeStruct((req.shape[0], CAP) + key_blocks.shape[1:], bf16),
        scratch_shapes=[pltpu.SemaphoreType.DMA],
        compiler_params=SMALL,
        name="pack_blocks",
    )(req, key_blocks)


def spread_kernel(own_ref, top_ref, bottom_ref, left_ref, right_ref, prop_ref, out_ref, rows_ref, side_ref, high_ref, low_ref, *, columns):
    pixels, _ = own_ref.shape
    sides = left_ref.shape[0]
    pad = side_ref.shape[0] // 2
    rows_ref[0:columns] = top_ref[...]
    rows_ref[columns : columns + pixels] = own_ref[...]
    rows_ref[columns + pixels :] = bottom_ref[...]
    side_ref[...] = jnp.zeros_like(side_ref)
    side_ref[0:sides] = left_ref[...]
    side_ref[pad : pad + sides] = right_ref[...]
    total = rows_ref.shape[0]
    weight = prop_ref[...]
    carried = jnp.dot(rows_ref[...], weight, preferred_element_type=f32)
    high = carried.astype(bf16)
    high_ref[0:total] = high
    low_ref[0:total] = (carried - high.astype(f32)).astype(bf16)
    carried = jnp.dot(side_ref[...], weight, preferred_element_type=f32)
    high = carried.astype(bf16)
    high_ref[total:] = high
    low_ref[total:] = (carried - high.astype(f32)).astype(bf16)

    size = 2 * columns
    reach = 4 * columns
    pix = lax.broadcasted_iota(jnp.int32, (size, reach), 0)
    oth = lax.broadcasted_iota(jnp.int32, (size, reach), 1)
    apart = oth // columns - pix // columns
    across = oth % columns - pix % columns
    near = (apart >= 0) & (apart <= 2) & (across >= -1) & (across <= 1)
    spix = lax.broadcasted_iota(jnp.int32, (size, 2 * pad), 0)
    soth = lax.broadcasted_iota(jnp.int32, (size, 2 * pad), 1)
    srow = jnp.where(soth < pad, soth, soth - pad) - spix // columns
    edge = jnp.where(soth < pad, 0, columns - 1) == spix % columns

    def weights(dots, keep):
        value = jnp.maximum(dots, 0.0)
        value = jnp.where(keep, value * value, 0.0)
        top = value.astype(bf16)
        return top, (value - top.astype(f32)).astype(bf16)

    def apply(pair, cut):
        top, rest = pair
        high, low = high_ref[cut], low_ref[cut]
        return (
            jnp.dot(top, high, preferred_element_type=f32)
            + jnp.dot(top, low, preferred_element_type=f32)
            + jnp.dot(rest, high, preferred_element_type=f32)
        )

    def block(index, carry):
        base = pl.multiple_of(index * size, size)
        own = own_ref[pl.ds(base, size)]
        around = pl.ds(base, reach)
        main = weights(transposed_dot(own, rows_ref[around]), near)
        shifted = srow - 2 * index
        keep = edge & (shifted >= 0) & (shifted <= 2)
        side = weights(transposed_dot(own, side_ref[...]), keep)
        spread = apply(main, around) + apply(side, pl.ds(total, 2 * pad))
        out_ref[pl.ds(base, size)] = normalize(spread).astype(bf16)
        return carry

    lax.fori_loop(0, pixels // size, block, 0)


def propagate(own, top, bottom, left, right, w_prop, columns):
    pixels, width = own.shape
    pad = -(-left.shape[0] // 16) * 16
    total = pixels + 2 * columns
    return pl.pallas_call(
        functools.partial(spread_kernel, columns=columns),
        in_specs=[VMEM] * 6,
        out_specs=VMEM,
        out_shape=jax.ShapeDtypeStruct((pixels, width), bf16),
        scratch_shapes=[
            pltpu.VMEM((total, width), bf16),
            pltpu.VMEM((2 * pad, width), bf16),
            pltpu.VMEM((total + 2 * pad, width), bf16),
            pltpu.VMEM((total + 2 * pad, width), bf16),
        ],
        compiler_params=SMALL,
        name="propagate",
    )(own, top, bottom, left, right, w_prop)


def loss_kernel(slot_ref, query_ref, keys_ref, partner_ref, mask_ref, out_ref):
    _, columns = out_ref.shape
    pixels, _ = query_ref.shape
    size = 2 * columns
    blocks = pixels // size
    per = slot_ref.shape[0] // blocks
    here = lax.broadcasted_iota(jnp.int32, (size, size), 0)
    there = lax.broadcasted_iota(jnp.int32, (size, size), 1)
    mirrored = (here // columns == there // columns) & (
        here % columns + there % columns == columns - 1
    )
    for block in range(blocks):
        query = query_ref[block * size : (block + 1) * size]
        match = transposed_dot(partner_ref[block * size : (block + 1) * size], query)
        match = jnp.sum(jnp.where(mirrored, match, 0.0), axis=0, keepdims=True)
        positive = match * inverse_divisor
        total = jnp.exp(positive)
        for n in range(per):
            keys = keys_ref[slot_ref[block * per + n]]
            logits = transposed_dot(keys, query) * inverse_divisor
            total = total + jnp.sum(jnp.exp(logits), axis=0, keepdims=True)
        loss = jnp.log(total) - positive
        for row in range(2):
            at = slice(2 * block + row, 2 * block + row + 1)
            piece = loss[:, row * columns : (row + 1) * columns]
            out_ref[at, :] = mask_ref[at, :].astype(f32) * piece


def loss_of(slot, query, received, partner, mask):
    return pl.pallas_call(
        loss_kernel,
        in_specs=[SMEM, VMEM, VMEM, VMEM, VMEM],
        out_specs=VMEM,
        out_shape=jax.ShapeDtypeStruct(mask.shape, f32),
        compiler_params=SMALL,
        name="loss_blocks",
    )(slot, query, received, partner, mask)


def shifted(value, axis):
    devices = lax.axis_size(axis)
    up = [(i, i + 1) for i in range(devices - 1)]
    return lax.ppermute(value[0], axis, up), lax.ppermute(value[1], axis, [(j, i) for i, j in up])


def per_device(feat_query, feat_key, w_hidden, w_out, w_prop, valid_mask, neg_shard, neg_block):
    height, columns, _ = feat_query.shape
    pixels = height * columns
    per_tile = pixels // 128
    shards = lax.axis_size("rows")
    cols = lax.axis_size("cols")
    want, slot = plan_slots(neg_shard, neg_block, shards)
    req = lax.all_to_all(want, "rows", 0, 0, tiled=True)
    key_map = project(feat_key, w_hidden, w_out)
    width = key_map.shape[-1]
    send = pack(req, key_map.reshape(per_tile, 128, width))
    received = lax.all_to_all(send, "rows", 0, 0, tiled=True)
    partner = lax.ppermute(key_map, "cols", [(i, cols - 1 - i) for i in range(cols)])
    feat_query, _ = lax.optimization_barrier((feat_query, send))
    query = project(feat_query, w_hidden, w_out)
    query_map = query.reshape(height, columns, width)
    top, bottom = shifted((query_map[-1], query_map[0]), "rows")
    first = jnp.concatenate([top[None, 0], query_map[:, 0], bottom[None, 0]])
    last = jnp.concatenate([top[None, -1], query_map[:, -1], bottom[None, -1]])
    left, right = shifted((last, first), "cols")
    propagated = propagate(query, top, bottom, left, right, w_prop, columns)
    return loss_of(
        slot, propagated, received.reshape(shards * CAP, 128, width), partner, valid_mask
    )


def solution(mesh):
    in_specs = (
        P("rows", "cols", None),
        P("rows", "cols", None),
        P(),
        P(),
        P(),
        P("rows", "cols"),
        P("rows", "cols", None, None),
        P("rows", "cols", None, None),
    )
    out_specs = P("rows", "cols")
    return jax.shard_map(
        per_device, mesh=mesh, in_specs=in_specs, out_specs=out_specs, check_vma=False
    )
```

time: 112 us -> 91.9 us (0.82)
  the two profiles are of different devices: /device:TPU:1 before, /device:TPU:40 now
where the time goes in v1:
time: 91.9 us; the launch traced here: 91.1 us
  Pallas kernels  46.1 us (50%)
  starting transfers between devices  29.8 us (32%)
  waiting for transfers between devices  9.78 us (11%)
  local copies, waits for them, and re-layouts  5.19 us (6%)
    pallas_call x2, Pallas kernels, project(): pl.pallas_call(project_kernel, grid=(pixels // ROWS,), in_specs=[pl.Block...  36.3 us
    all_to_all x1, starting transfers between devices, per_device(): req = lax.all_to_all(want, 'rows', 0, 0, tiled=True)  7.18 us
    ppermute x2, starting transfers between devices, shifted(): lax.ppermute(value[1], axis, [(j, i) for i, j in up])  6.97 us
    all_to_all x1, starting transfers between devices, per_device(): received = lax.all_to_all(send, 'rows', 0, 0, tiled=True)  6.63 us
    ppermute x2, waiting for transfers between devices, shifted(): lax.ppermute(value[0], axis, up)  5.69 us
    ppermute x2, starting transfers between devices, shifted(): lax.ppermute(value[0], axis, up)  5.37 us
    pallas_call x1, Pallas kernels, propagate(): pl.pallas_call(functools.partial(spread_kernel, columns=columns), in_spec...  4.74 us
    ppermute x2, waiting for transfers between devices, shifted(): lax.ppermute(value[1], axis, [(j, i) for i, j in up])  4.09 us
  transfers between devices with their start and end apart: 7, of which 2 were waited for; matrix products, arithmetic and copies ran while one was open for 2% of the time, Pallas kernels for 47%

profile of v1, /device:TPU:40, one launch (start us, length us, event | category | flops | bytes accessed | tf_op | source)
XLA Modules:
  0.0 91.1 jit_solution(10389613615441721082)
XLA Ops:
  0.0 0.7 copy-done.4
  0.7 0.0 copy-start.5
  0.7 0.7 copy-done.5
  1.4 1.3 %plan_slots.1 = (s32[16,1,128]{2,1,0:T(1,128)}, s32[16]{0:T(128)S(1)}) custom-call(s32[1,1,2,8]{3,2,1,0:T(2,128)S(1)} %bitcast.16, s32[1,1,2,8]{3,2,1,0:T(2,128)S(1)} %bitcast.17), custom_call_target="tpu_custom_call" | custom-call | tf_op jit(solution)/shard_map/plan_slots/pallas_call | solution.py:54
  2.7 7.2 %all-to-all-start = ((s32[16,1,128]{2,1,0:T(1,128)}), s32[16,1,128]{2,1,0:T(1,128)S(1)}, u32[]{:S(2)}, u32[]{:S(2)}) async-start(s32[16,1,128]{2,1,0:T(1,128)} %get-tuple-element.9), calls=%async_computation | async-start | bytes 16384 | tf_op jit(solution)/shard_map/all_to_all | solution.py:292
  9.9 18.1 %shard_map.82 = bf16[1024,256]{1,0:T(8,128)(2,1)} custom-call(bf16[1024,2048]{1,0:T(8,128)(2,1)} %bitcast.20, bf16[2048,2048]{1,0:T(8,128)(2,1)} %hidden_hbm.3, bf16[2048,256]{1,0:T(8,128)(2,1)} %out_hbm.3), custom_call_target="tpu_custom_call" | custom-call | flops 9663676416 | bytes 13631488 | tf_op jit(solution)/shard_map/pallas_call | solution.py:117
  28.0 3.6 %collective-permute-start.4 = (bf16[1024,256]{1,0:T(8,128)(2,1)}, bf16[1024,256]{1,0:T(8,128)(2,1)S(1)}, u32[]{:S(2)}, u32[]{:S(2)}) collective-permute-start(bf16[1024,256]{1,0:T(8,128)(2,1)} %shard_map.82), channel_id=1, source_target_pairs={{0,7},{1,6},{2,5},{3,4},{4,3},{5,2},{6,1},{7,0},{8,15},{9,14},{10,... | collective-permute-start | bytes 1572872 | tf_op jit(solution)/shard_map/ppermute | solution.py:297
  31.6 0.0 all-to-all-done.req_ref
  31.6 0.0 copy-start.1
  31.6 1.1 %copy-done.1 = bf16[1024,256]{1,0:T(8,128)(2,1)S(1)} copy-done((bf16[1024,256]{1,0:T(8,128)(2,1)S(1)}, bf16[1024,256]{1,0:T(8,128)(2,1)}, u32[]{:S(2)}) %copy-start.1) | copy-done | bytes 524312
  32.7 2.0 %pack_blocks.1 = bf16[16,2,128,256]{3,2,1,0:T(8,128)(2,1)} custom-call(s32[16,1,128]{2,1,0:T(1,128)S(1)} %all-to-all-done.req_ref, bf16[8,128,256]{2,1,0:T(8,128)(2,1)S(1)} %bitcast.15), custom_call_target="tpu_custom_call" | custom-call | tf_op jit(solution)/shard_map/pack_blocks/pallas_call | solution.py:146
  34.7 6.6 %all-to-all-start.1 = ((bf16[16,2,128,256]{3,2,1,0:T(8,128)(2,1)}), bf16[16,2,128,256]{3,2,1,0:T(8,128)(2,1)S(1)}, u32[]{:S(2)}, u32[]{:S(2)}) async-start(bf16[16,2,128,256]{3,2,1,0:T(8,128)(2,1)} %pack_blocks.1), calls=%async_computation.1 | async-start | bytes 4194304 | tf_op jit(solution)/shard_map/all_to_all | solution.py:296
  41.3 0.0 copy-start.2
  41.4 0.0 copy-start.3
  41.4 18.1 %shard_map.83.own_ref = bf16[1024,256]{1,0:T(8,128)(2,1)} custom-call(bf16[1024,2048]{1,0:T(8,128)(2,1)} %bitcast.21, bf16[2048,2048]{1,0:T(8,128)(2,1)} %hidden_hbm.3, bf16[2048,256]{1,0:T(8,128)(2,1)} %out_hbm.3), custom_call_target="tpu_custom_call" | custom-call | flops 9663676416 | bytes 13631488 | tf_op jit(solution)/shard_map/pallas_call | solution.py:117
  59.5 0.8 fusion.1
  60.3 4.6 %collective-permute-start.1 = (bf16[64,256]{1,0:T(8,128)(2,1)S(1)}, bf16[64,256]{1,0:T(8,128)(2,1)S(1)}, u32[]{:S(2)}, u32[]{:S(2)}) collective-permute-start(bf16[64,256]{1,0:T(8,128)(2,1)S(1)} %get-tuple-element.13), channel_id=1, source_target_pairs={{8,0},{16,8},{24,16},{32,24},{40,32},{48,40},{56,48},{64,56},{72,6... | collective-permute-start | bytes 98312 | tf_op jit(solution)/shard_map/ppermute | solution.py:282
  64.9 0.9 fusion
  65.8 1.9 %collective-permute-start = (bf16[64,256]{1,0:T(8,128)(2,1)S(1)}, bf16[64,256]{1,0:T(8,128)(2,1)S(1)}, u32[]{:S(2)}, u32[]{:S(2)}) collective-permute-start(bf16[64,256]{1,0:T(8,128)(2,1)S(1)} %get-tuple-element.14), channel_id=1, source_target_pairs={{0,8},{8,16},{16,24},{24,32},{32,40},{40,48},{48,56},{56,64},{64,7... | collective-permute-start | bytes 98312 | tf_op jit(solution)/shard_map/ppermute | solution.py:282
  67.8 0.0 collective-permute-done.1.bottom_ref
  67.8 5.7 %collective-permute-done.top_ref = bf16[64,256]{1,0:T(8,128)(2,1)S(1)} collective-permute-done((bf16[64,256]{1,0:T(8,128)(2,1)S(1)}, bf16[64,256]{1,0:T(8,128)(2,1)S(1)}, u32[]{:S(2)}, u32[]{:S(2)}) %collective-permute-start) | collective-permute-done | bytes 32800 | tf_op jit(solution)/shard_map/ppermute | solution.py:282
  73.5 3.5 %collective-permute-start.2 = (bf16[18,256]{1,0:T(8,128)(2,1)S(1)}, bf16[18,256]{1,0:T(8,128)(2,1)S(1)}, u32[]{:S(2)}, u32[]{:S(2)}) collective-permute-start(bf16[18,256]{1,0:T(8,128)(2,1)S(1)} %pad_maximum_fusion), channel_id=1, source_target_pairs={{0,1},{1,2},{2,3},{3,4},{4,5},{5,6},{6,7},{8,9},{9,10},{10,11},{11... | collective-permute-start | bytes 27656 | tf_op jit(solution)/shard_map/ppermute | solution.py:282
  77.0 2.4 %collective-permute-start.3 = (bf16[18,256]{1,0:T(8,128)(2,1)S(1)}, bf16[18,256]{1,0:T(8,128)(2,1)S(1)}, u32[]{:S(2)}, u32[]{:S(2)}) collective-permute-start(bf16[18,256]{1,0:T(8,128)(2,1)S(1)} %pad_maximum_fusion.1), channel_id=1, source_target_pairs={{1,0},{2,1},{3,2},{4,3},{5,4},{6,5},{7,6},{9,8},{10,9},{11,10},{12... | collective-permute-start | bytes 27656 | tf_op jit(solution)/shard_map/ppermute | solution.py:282
  79.4 0.0 collective-permute-done.2.left_ref
  79.4 4.1 %collective-permute-done.3.right_ref = bf16[18,256]{1,0:T(8,128)(2,1)S(1)} collective-permute-done((bf16[18,256]{1,0:T(8,128)(2,1)S(1)}, bf16[18,256]{1,0:T(8,128)(2,1)S(1)}, u32[]{:S(2)}, u32[]{:S(2)}) %collective-permute-start.3) | collective-permute-done | bytes 9248 | tf_op jit(solution)/shard_map/ppermute | solution.py:282
  83.5 0.0 copy-done.2
  83.5 1.0 %copy-done = bf16[1024,256]{1,0:T(8,128)(2,1)S(1)} copy-done((bf16[1024,256]{1,0:T(8,128)(2,1)S(1)}, bf16[1024,256]{1,0:T(8,128)(2,1)}, u32[]{:S(2)}) %copy-start) | copy-done | bytes 524312
  84.5 4.7 %propagate.1.query_ref = bf16[1024,256]{1,0:T(8,128)(2,1)S(1)} custom-call(bf16[1024,256]{1,0:T(8,128)(2,1)S(1)} %copy-done, bf16[64,256]{1,0:T(8,128)(2,1)S(1)} %collective-permute-done.top_ref, bf16[64,256]{1,0:T(8,128)(2,1)S(1)} %collective-permute-done.1.bottom_ref, bf16[18,256]{1,0:T(8,128)(2,1)S(1)} %collective-permute-done.2.left_ref, ...), custom_call_target="tpu_custom_call" | custom-call | tf_op jit(solution)/shard_map/propagate/pallas_call | solution.py:224
  89.2 0.0 collective-permute-done.4.partner_ref
  89.3 0.0 all-to-all-done.1
  89.3 0.0 copy-done.3
  89.3 1.8 %loss_blocks.1 = f32[16,64]{1,0:T(8,128)} custom-call(s32[16]{0:T(128)S(1)} %get-tuple-element.8.slot_ref, bf16[1024,256]{1,0:T(8,128)(2,1)S(1)} %propagate.1.query_ref, bf16[32,128,256]{2,1,0:T(8,128)(2,1)S(1)} %bitcast.13, bf16[1024,256]{1,0:T(8,128)(2,1)S(1)} %collective-permute-done.4.partner_ref, s32[16,64]{1,0:T(8,128)S(1)} %copy-done.3), custom_call_target="tpu_custom_call" | custom-call | tf_op jit(solution)/shard_map/loss_blocks/pallas_call | solution.py:269
  (8 shorter events, 0.1 us)
Async XLA Ops:
  0.0 0.7 copy-start.4
  0.7 0.7 copy-start.5
  2.7 28.9 %all-to-all-start = ((s32[16,1,128]{2,1,0:T(1,128)}), s32[16,1,128]{2,1,0:T(1,128)S(1)}, u32[]{:S(2)}, u32[]{:S(2)}) async-start(s32[16,1,128]{2,1,0:T(1,128)} %get-tuple-element.9), calls=%async_computation | async-start | bytes 16384 | tf_op jit(solution)/shard_map/all_to_all | solution.py:292
  28.0 61.3 %collective-permute-start.4 = (bf16[1024,256]{1,0:T(8,128)(2,1)}, bf16[1024,256]{1,0:T(8,128)(2,1)S(1)}, u32[]{:S(2)}, u32[]{:S(2)}) collective-permute-start(bf16[1024,256]{1,0:T(8,128)(2,1)} %shard_map.82), channel_id=1, source_target_pairs={{0,7},{1,6},{2,5},{3,4},{4,3},{5,2},{6,1},{7,0},{8,15},{9,14},{10,... | collective-permute-start | bytes 1572872 | tf_op jit(solution)/shard_map/ppermute | solution.py:297
  31.6 1.1 %copy-start.1 = (bf16[1024,256]{1,0:T(8,128)(2,1)S(1)}, bf16[1024,256]{1,0:T(8,128)(2,1)}, u32[]{:S(2)}) copy-start(bf16[1024,256]{1,0:T(8,128)(2,1)} %shard_map.82) | copy-start | bytes 1572868
  34.7 54.5 %all-to-all-start.1 = ((bf16[16,2,128,256]{3,2,1,0:T(8,128)(2,1)}), bf16[16,2,128,256]{3,2,1,0:T(8,128)(2,1)S(1)}, u32[]{:S(2)}, u32[]{:S(2)}) async-start(bf16[16,2,128,256]{3,2,1,0:T(8,128)(2,1)} %pack_blocks.1), calls=%async_computation.1 | async-start | bytes 4194304 | tf_op jit(solution)/shard_map/all_to_all | solution.py:296
  41.3 42.1 %copy-start.2 = (bf16[256,256]{1,0:T(8,128)(2,1)S(1)}, bf16[256,256]{1,0:T(8,128)(2,1)}, u32[]{:S(2)}) copy-start(bf16[256,256]{1,0:T(8,128)(2,1)} %prop_ref.1) | copy-start | bytes 393220
  41.4 47.9 %copy-start.3 = (s32[16,64]{1,0:T(8,128)S(1)}, s32[16,64]{1,0:T(8,128)}, u32[]{:S(2)}) copy-start(s32[16,64]{1,0:T(8,128)} %mask_ref.1) | copy-start | bytes 12292
  60.3 7.5 %collective-permute-start.1 = (bf16[64,256]{1,0:T(8,128)(2,1)S(1)}, bf16[64,256]{1,0:T(8,128)(2,1)S(1)}, u32[]{:S(2)}, u32[]{:S(2)}) collective-permute-start(bf16[64,256]{1,0:T(8,128)(2,1)S(1)} %get-tuple-element.13), channel_id=1, source_target_pairs={{8,0},{16,8},{24,16},{32,24},{40,32},{48,40},{56,48},{64,56},{72,6... | collective-permute-start | bytes 98312 | tf_op jit(solution)/shard_map/ppermute | solution.py:282
  65.8 7.6 %collective-permute-start = (bf16[64,256]{1,0:T(8,128)(2,1)S(1)}, bf16[64,256]{1,0:T(8,128)(2,1)S(1)}, u32[]{:S(2)}, u32[]{:S(2)}) collective-permute-start(bf16[64,256]{1,0:T(8,128)(2,1)S(1)} %get-tuple-element.14), channel_id=1, source_target_pairs={{0,8},{8,16},{16,24},{24,32},{32,40},{40,48},{48,56},{56,64},{64,7... | collective-permute-start | bytes 98312 | tf_op jit(solution)/shard_map/ppermute | solution.py:282
  73.5 5.9 %collective-permute-start.2 = (bf16[18,256]{1,0:T(8,128)(2,1)S(1)}, bf16[18,256]{1,0:T(8,128)(2,1)S(1)}, u32[]{:S(2)}, u32[]{:S(2)}) collective-permute-start(bf16[18,256]{1,0:T(8,128)(2,1)S(1)} %pad_maximum_fusion), channel_id=1, source_target_pairs={{0,1},{1,2},{2,3},{3,4},{4,5},{5,6},{6,7},{8,9},{9,10},{10,11},{11... | collective-permute-start | bytes 27656 | tf_op jit(solution)/shard_map/ppermute | solution.py:282
  77.0 6.5 %collective-permute-start.3 = (bf16[18,256]{1,0:T(8,128)(2,1)S(1)}, bf16[18,256]{1,0:T(8,128)(2,1)S(1)}, u32[]{:S(2)}, u32[]{:S(2)}) collective-permute-start(bf16[18,256]{1,0:T(8,128)(2,1)S(1)} %pad_maximum_fusion.1), channel_id=1, source_target_pairs={{1,0},{2,1},{3,2},{4,3},{5,4},{6,5},{7,6},{9,8},{10,9},{11,10},{12... | collective-permute-start | bytes 27656 | tf_op jit(solution)/shard_map/ppermute | solution.py:282
  83.5 1.0 %copy-start = (bf16[1024,256]{1,0:T(8,128)(2,1)S(1)}, bf16[1024,256]{1,0:T(8,128)(2,1)}, u32[]{:S(2)}) copy-start(bf16[1024,256]{1,0:T(8,128)(2,1)} %shard_map.83.own_ref) | copy-start | bytes 1572868

commit v2 on v1

--- a/solution.py
+++ b/solution.py
@@ -64,74 +64,115 @@
     )(neg_shard.transpose(0, 1, 3, 2), neg_block.transpose(0, 1, 3, 2))
 
 
-ROWS = 256
-PARTS = 8
-
-
-def project_kernel(feat_ref, hidden_hbm, out_hbm, map_ref, hidden_w, out_w, sem):
-    step = pl.program_id(0)
-    span = hidden_w.shape[1] // PARTS
-
-    def piece(index):
-        cut = pl.ds(index * span, span)
-        return pltpu.make_async_copy(hidden_hbm.at[:, cut], hidden_w.at[:, cut], sem.at[index])
-
-    def tail():
-        return pltpu.make_async_copy(out_hbm, out_w, sem.at[PARTS])
-
-    def finish(raw):
-        map_ref[...] = normalize(raw).astype(map_ref.dtype)
-
-    def layer(cut):
-        hidden = jnp.dot(feat_ref[...], hidden_w[:, cut], preferred_element_type=f32)
-        hidden = jnp.maximum(hidden, 0.0).astype(bf16)
-        return jnp.dot(hidden, out_w[cut, :], preferred_element_type=f32)
-
-    @pl.when(step == 0)
-    def _():
-        piece(0).start()
-        piece(1).start()
-        tail().start()
-        total = None
-        for index in range(0, PARTS, 2):
-            piece(index).wait()
-            piece(index + 1).wait()
-            if index == 0:
-                tail().wait()
-            if index + 2 < PARTS:
-                piece(index + 2).start()
-                piece(index + 3).start()
-            term = layer(pl.ds(index * span, 2 * span))
-            total = term if total is None else total + term
-        finish(total)
-
-    @pl.when(step > 0)
-    def _():
-        finish(layer(pl.ds(0, hidden_w.shape[1])))
-
-
-def project(feat_map, w_hidden, w_out):
+PARTS = 4
+STRIP = 16
+
+
+def project_kernel(*refs, edges):
+    feat_hbm, hidden_hbm, out_hbm = refs[:3]
+    if edges:
+        other_hbm, map_ref, first_row, last_row, first_col, last_col = refs[3:9]
+        feat, total, hidden_w, out_w, sems, strips = refs[9:]
+        height, columns, _ = other_hbm.shape
+    else:
+        map_ref, feat, total, hidden_w, out_w, sems = refs[3:]
+    pixels, channels = feat_hbm.shape
+    half = pixels // 2
+    span = channels // PARTS
+    cuts = [slice(part * span, (part + 1) * span) for part in range(PARTS)]
+
+    def copy(source, target, sem):
+        return pltpu.make_async_copy(source, target, sems.at[sem])
+
+    feats = [copy(feat_hbm.at[0:half, c], feat.at[0:half, c], i) for i, c in enumerate(cuts)]
+    pieces = [copy(hidden_hbm.at[c], hidden_w.at[c], PARTS + i) for i, c in enumerate(cuts)]
+    later = [
+        copy(out_hbm, out_w, 2 * PARTS),
+        copy(feat_hbm.at[half:pixels], feat.at[half:pixels], 2 * PARTS + 1),
+    ]
+    if edges:
+        top = pixels + columns
+        later += [
+            copy(other_hbm.at[0], feat.at[pixels:top], 2 * PARTS + 2),
+            copy(other_hbm.at[height - 1], feat.at[top : top + columns], 2 * PARTS + 3),
+            copy(other_hbm.at[:, 0:STRIP], strips.at[0], 2 * PARTS + 4),
+            copy(other_hbm.at[:, columns - STRIP : columns], strips.at[1], 2 * PARTS + 5),
+        ]
+    for first, second in zip(feats, pieces):
+        first.start()
+        second.start()
+    for one in later:
+        one.start()
+    for part, cut in enumerate(cuts):
+        feats[part].wait()
+        pieces[part].wait()
+        term = jnp.dot(feat[0:half, cut], hidden_w[cut, :], preferred_element_type=f32)
+        if part == 0:
+            total[...] = term
+        elif part < PARTS - 1:
+            total[...] += term
+        else:
+            hidden = jnp.maximum(total[...] + term, 0.0).astype(bf16)
+    later[0].wait()
+    raw = jnp.dot(hidden, out_w[...], preferred_element_type=f32)
+    map_ref[0:half] = normalize(raw).astype(bf16)
+    for one in later[1:]:
+        one.wait()
+    if edges:
+        row = lax.broadcasted_iota(jnp.int32, (height, height * STRIP), 0)
+        place = lax.broadcasted_iota(jnp.int32, (height, height * STRIP), 1)
+        base = pixels + 2 * columns
+        for side, offset in ((0, 0), (1, STRIP - 1)):
+            pick = (place == row * STRIP + offset).astype(f32).astype(bf16)
+            strip = strips[side].reshape(height * STRIP, channels)
+            taken = jnp.dot(pick, strip, preferred_element_type=f32).astype(bf16)
+            feat[base + side * height : base + (side + 1) * height] = taken
+    hidden = jnp.dot(feat[half:], hidden_w[...], preferred_element_type=f32)
+    hidden = jnp.maximum(hidden, 0.0).astype(bf16)
+    done = normalize(jnp.dot(hidden, out_w[...], preferred_element_type=f32)).astype(bf16)
+    map_ref[half:pixels] = done[0 : pixels - half]
+    if edges:
+        place = pixels - half
+        for ref in (first_row, last_row, first_col, last_col):
+            ref[...] = done[place : place + ref.shape[0]]
+            place += ref.shape[0]
+
+
+def project(feat_map, w_hidden, w_out, other=None):
     height, columns, channels = feat_map.shape
     pixels = height * columns
     hidden, width = w_out.shape
-    return pl.pallas_call(
-        project_kernel,
-        grid=(pixels // ROWS,),
-        in_specs=[pl.BlockSpec((ROWS, channels), lambda i: (i, 0)), ANY, ANY],
-        out_specs=pl.BlockSpec((ROWS, width), lambda i: (i, 0)),
-        out_shape=jax.ShapeDtypeStruct((pixels, width), bf16),
+    operands = [feat_map.reshape(pixels, channels), w_hidden, w_out]
+    outputs = [jax.ShapeDtypeStruct((pixels, width), bf16)]
+    extra = 0
+    scratch = []
+    if other is not None:
+        operands.append(other)
+        for size in (columns, columns, height, height):
+            outputs.append(jax.ShapeDtypeStruct((size, width), bf16))
+            extra += size
+        scratch = [pltpu.VMEM((2, height, STRIP, channels), bf16)]
+    results = pl.pallas_call(
+        functools.partial(project_kernel, edges=other is not None),
+        in_specs=[ANY] * len(operands),
+        out_specs=[VMEM] * len(outputs),
+        out_shape=outputs,
         scratch_shapes=[
+            pltpu.VMEM((pixels + extra, channels), bf16),
+            pltpu.VMEM((pixels // 2, hidden), f32),
             pltpu.VMEM((channels, hidden), bf16),
             pltpu.VMEM((hidden, width), bf16),
-            pltpu.SemaphoreType.DMA((PARTS + 1,)),
+            pltpu.SemaphoreType.DMA((2 * PARTS + 6,)),
+            *scratch,
         ],
         compiler_params=pltpu.CompilerParams(vmem_limit_bytes=LIMIT),
         cost_estimate=pl.CostEstimate(
-            flops=2 * pixels * hidden * (channels + width),
+            flops=2 * (pixels + extra) * hidden * (channels + width),
             bytes_accessed=2 * (pixels * channels + hidden * (channels + width)),
             transcendentals=0,
         ),
-    )(feat_map.reshape(pixels, channels), w_hidden, w_out)
+    )(*operands)
+    return results if other is not None else results[0]
 
 
 def pack_kernel(req_ref, keys_ref, out_ref, sem):
@@ -290,18 +331,19 @@
     cols = lax.axis_size("cols")
     want, slot = plan_slots(neg_shard, neg_block, shards)
     req = lax.all_to_all(want, "rows", 0, 0, tiled=True)
-    key_map = project(feat_key, w_hidden, w_out)
+    key_map, first_row, last_row, first_col, last_col = project(
+        feat_key, w_hidden, w_out, feat_query
+    )
     width = key_map.shape[-1]
+    top, bottom = shifted((last_row, first_row), "rows")
     send = pack(req, key_map.reshape(per_tile, 128, width))
     received = lax.all_to_all(send, "rows", 0, 0, tiled=True)
     partner = lax.ppermute(key_map, "cols", [(i, cols - 1 - i) for i in range(cols)])
+    first = jnp.concatenate([top[:1], first_col, bottom[:1]])
+    last = jnp.concatenate([top[-1:], last_col, bottom[-1:]])
+    left, right = shifted((last, first), "cols")
     feat_query, _ = lax.optimization_barrier((feat_query, send))
     query = project(feat_query, w_hidden, w_out)
-    query_map = query.reshape(height, columns, width)
-    top, bottom = shifted((query_map[-1], query_map[0]), "rows")
-    first = jnp.concatenate([top[None, 0], query_map[:, 0], bottom[None, 0]])
-    last = jnp.concatenate([top[None, -1], query_map[:, -1], bottom[None, -1]])
-    left, right = shifted((last, first), "cols")
     propagated = propagate(query, top, bottom, left, right, w_prop, columns)
     return loss_of(
         slot, propagated, received.reshape(shards * CAP, 128, width), partner, valid_mask

time: 91.9 us -> 108 us (1.18)
  the two profiles are of different devices: /device:TPU:40 before, /device:TPU:1 now
where the time goes in v2:
time: 108 us; the launch traced here: 107 us
  Pallas kernels  41.1 us (38%)
  starting transfers between devices  30.9 us (29%)
  waiting for transfers between devices  29.1 us (27%)
  local copies, waits for them, and re-layouts  5.3 us (5%)
    pallas_call x2, Pallas kernels, project(): pl.pallas_call(functools.partial(project_kernel, edges=other is not None)...  31.2 us
    ppermute x2, waiting for transfers between devices, shifted(): lax.ppermute(value[0], axis, up)  26.2 us
    all_to_all x1, starting transfers between devices, per_device(): req = lax.all_to_all(want, 'rows', 0, 0, tiled=True)  9.46 us
    ppermute x2, starting transfers between devices, shifted(): lax.ppermute(value[0], axis, up)  8.14 us
    all_to_all x1, starting transfers between devices, per_device(): received = lax.all_to_all(send, 'rows', 0, 0, tiled=True)  7.24 us
    unnamed x26, local copies, waits for them, and re-layouts  5.29 us
    pallas_call x1, Pallas kernels, propagate(): pl.pallas_call(functools.partial(spread_kernel, columns=columns), in_spec...  4.74 us
    ppermute x2, starting transfers between devices, shifted(): lax.ppermute(value[1], axis, [(j, i) for i, j in up])  3.38 us
  transfers between devices with their start and end apart: 7, of which 2 were waited for; matrix products, arithmetic and copies ran while one was open for 0% of the time, Pallas kernels for 34%

profile of v2, /device:TPU:1, one launch (start us, length us, event | category | flops | bytes accessed | tf_op | source)
XLA Modules:
  0.0 106.6 jit_solution(14701085423273519798)
XLA Ops:
  0.0 0.7 copy-done.7
  0.7 0.7 copy-done.8
  1.4 1.3 %plan_slots.1 = (s32[16,1,128]{2,1,0:T(1,128)}, s32[16]{0:T(128)S(1)}) custom-call(s32[1,1,2,8]{3,2,1,0:T(2,128)S(1)} %bitcast.8, s32[1,1,2,8]{3,2,1,0:T(2,128)S(1)} %bitcast.9), custom_call_target="tpu_custom_call" | custom-call | tf_op jit(solution)/shard_map/plan_slots/pallas_call | solution.py:54
  2.7 9.5 %all-to-all-start = ((s32[16,1,128]{2,1,0:T(1,128)}), s32[16,1,128]{2,1,0:T(1,128)S(1)}, u32[]{:S(2)}, u32[]{:S(2)}) async-start(s32[16,1,128]{2,1,0:T(1,128)} %get-tuple-element.14), calls=%async_computation | async-start | bytes 16384 | tf_op jit(solution)/shard_map/all_to_all | solution.py:333
  12.2 16.6 %shard_map.82 = (bf16[1024,256]{1,0:T(8,128)(2,1)}, bf16[64,256]{1,0:T(8,128)(2,1)}, bf16[64,256]{1,0:T(8,128)(2,1)}, bf16[16,256]{1,0:T(8,128)(2,1)}, bf16[16,256]{1,0:T(8,128)(2,1)}) custom-call(bf16[1024,2048]{1,0:T(8,128)(2,1)} %bitcast.10, bf16[2048,2048]{1,0:T(8,128)(2,1)} %refs_1_.3, bf16[2048,256]{1,0:T(8,128)(2,1)} %refs_2_.3, ...), custom_call_target="tpu_custom_call" | custom-call | flops 11173625856 | bytes 13631488 | tf_op jit(solution)/shard_map/pallas_call | solution.py:155
  28.8 0.0 all-to-all-done.req_ref
  28.8 1.0 copy-done
  29.8 2.0 %pack_blocks.1 = bf16[16,2,128,256]{3,2,1,0:T(8,128)(2,1)} custom-call(s32[16,1,128]{2,1,0:T(1,128)S(1)} %all-to-all-done.req_ref, bf16[8,128,256]{2,1,0:T(8,128)(2,1)S(1)} %bitcast.7), custom_call_target="tpu_custom_call" | custom-call | tf_op jit(solution)/shard_map/pack_blocks/pallas_call | solution.py:187
  31.9 7.2 %all-to-all-start.1 = ((bf16[16,2,128,256]{3,2,1,0:T(8,128)(2,1)}), bf16[16,2,128,256]{3,2,1,0:T(8,128)(2,1)S(1)}, u32[]{:S(2)}, u32[]{:S(2)}) async-start(bf16[16,2,128,256]{3,2,1,0:T(8,128)(2,1)} %pack_blocks.1), calls=%async_computation.1 | async-start | bytes 4194304 | tf_op jit(solution)/shard_map/all_to_all | solution.py:340
  39.1 5.0 %collective-permute-start = (bf16[64,256]{1,0:T(8,128)(2,1)S(1)}, bf16[64,256]{1,0:T(8,128)(2,1)S(1)}, u32[]{:S(2)}, u32[]{:S(2)}) collective-permute-start(bf16[64,256]{1,0:T(8,128)(2,1)S(1)} %copy-done.12), channel_id=1, source_target_pairs={{0,8},{8,16},{16,24},{24,32},{32,40},{40,48},{48,56},{56,64},{64,7... | collective-permute-start | bytes 98312 | tf_op jit(solution)/shard_map/ppermute | solution.py:323
  44.1 0.0 copy-done.1
  44.2 2.7 %collective-permute-start.4 = (bf16[1024,256]{1,0:T(8,128)(2,1)S(1)}, bf16[1024,256]{1,0:T(8,128)(2,1)S(1)}, u32[]{:S(2)}, u32[]{:S(2)}) collective-permute-start(bf16[1024,256]{1,0:T(8,128)(2,1)S(1)} %copy-done.1), channel_id=1, source_target_pairs={{0,7},{1,6},{2,5},{3,4},{4,3},{5,2},{6,1},{7,0},{8,15},{9,14},{10,... | collective-permute-start | bytes 1572872 | tf_op jit(solution)/shard_map/ppermute | solution.py:341
  46.8 1.9 %collective-permute-start.1 = (bf16[64,256]{1,0:T(8,128)(2,1)S(1)}, bf16[64,256]{1,0:T(8,128)(2,1)S(1)}, u32[]{:S(2)}, u32[]{:S(2)}) collective-permute-start(bf16[64,256]{1,0:T(8,128)(2,1)S(1)} %copy-done.11), channel_id=1, source_target_pairs={{8,0},{16,8},{24,16},{32,24},{40,32},{48,40},{56,48},{64,56},{72,6... | collective-permute-start | bytes 98312 | tf_op jit(solution)/shard_map/ppermute | solution.py:323
  48.7 26.2 %collective-permute-done.top_ref = bf16[64,256]{1,0:T(8,128)(2,1)S(1)} collective-permute-done((bf16[64,256]{1,0:T(8,128)(2,1)S(1)}, bf16[64,256]{1,0:T(8,128)(2,1)S(1)}, u32[]{:S(2)}, u32[]{:S(2)}) %collective-permute-start) | collective-permute-done | bytes 32800 | tf_op jit(solution)/shard_map/ppermute | solution.py:323
  75.0 2.8 %collective-permute-done.1.bottom_ref = bf16[64,256]{1,0:T(8,128)(2,1)S(1)} collective-permute-done((bf16[64,256]{1,0:T(8,128)(2,1)S(1)}, bf16[64,256]{1,0:T(8,128)(2,1)S(1)}, u32[]{:S(2)}, u32[]{:S(2)}) %collective-permute-start.1) | collective-permute-done | bytes 32800 | tf_op jit(solution)/shard_map/ppermute | solution.py:323
  77.8 0.0 copy-done.10
  77.8 3.1 %collective-permute-start.2 = (bf16[18,256]{1,0:T(8,128)(2,1)S(1)}, bf16[18,256]{1,0:T(8,128)(2,1)S(1)}, u32[]{:S(2)}, u32[]{:S(2)}) collective-permute-start(bf16[18,256]{1,0:T(8,128)(2,1)S(1)} %pad_maximum_fusion), channel_id=1, source_target_pairs={{0,1},{1,2},{2,3},{3,4},{4,5},{5,6},{6,7},{8,9},{9,10},{10,11},{11... | collective-permute-start | bytes 27656 | tf_op jit(solution)/shard_map/ppermute | solution.py:323
  81.0 1.5 %collective-permute-start.3 = (bf16[18,256]{1,0:T(8,128)(2,1)S(1)}, bf16[18,256]{1,0:T(8,128)(2,1)S(1)}, u32[]{:S(2)}, u32[]{:S(2)}) collective-permute-start(bf16[18,256]{1,0:T(8,128)(2,1)S(1)} %pad_maximum_fusion.1), channel_id=1, source_target_pairs={{1,0},{2,1},{3,2},{4,3},{5,4},{6,5},{7,6},{9,8},{10,9},{11,10},{12... | collective-permute-start | bytes 27656 | tf_op jit(solution)/shard_map/ppermute | solution.py:323
  82.4 0.0 copy-start.5
  82.4 0.0 copy-start.6
  82.5 14.6 %shard_map.83.own_ref = bf16[1024,256]{1,0:T(8,128)(2,1)} custom-call(bf16[1024,2048]{1,0:T(8,128)(2,1)} %bitcast.11, bf16[2048,2048]{1,0:T(8,128)(2,1)} %refs_1_.3, bf16[2048,256]{1,0:T(8,128)(2,1)} %refs_2_.3), custom_call_target="tpu_custom_call" | custom-call | flops 9663676416 | bytes 13631488 | tf_op jit(solution)/shard_map/pallas_call | solution.py:155
  97.1 0.0 collective-permute-done.2.left_ref
  97.1 0.0 collective-permute-done.3.right_ref
  97.1 0.0 copy-done.5
  97.1 0.0 copy-start.2
  97.1 1.0 copy-done.2
  98.2 4.7 %propagate.1.query_ref = bf16[1024,256]{1,0:T(8,128)(2,1)S(1)} custom-call(bf16[1024,256]{1,0:T(8,128)(2,1)S(1)} %copy-done.2, bf16[64,256]{1,0:T(8,128)(2,1)S(1)} %collective-permute-done.top_ref, bf16[64,256]{1,0:T(8,128)(2,1)S(1)} %collective-permute-done.1.bottom_ref, bf16[18,256]{1,0:T(8,128)(2,1)S(1)} %collective-permute-done.2.left_ref, ...), custom_call_target="tpu_custom_call" | custom-call | tf_op jit(solution)/shard_map/propagate/pallas_call | solution.py:265
  102.9 0.0 collective-permute-done.4.partner_ref
  102.9 0.8 copy-done.3
  103.7 0.0 all-to-all-done.1
  103.7 1.0 copy-done.4
  104.8 1.8 %loss_blocks.1 = f32[16,64]{1,0:T(8,128)} custom-call(s32[16]{0:T(128)S(1)} %get-tuple-element.13.slot_ref, bf16[1024,256]{1,0:T(8,128)(2,1)S(1)} %propagate.1.query_ref, bf16[32,128,256]{2,1,0:T(8,128)(2,1)S(1)} %bitcast.6, bf16[1024,256]{1,0:T(8,128)(2,1)S(1)} %copy-done.4, s32[16,64]{1,0:T(8,128)S(1)} %copy-done.6), custom_call_target="tpu_custom_call" | custom-call | tf_op jit(solution)/shard_map/loss_blocks/pallas_call | solution.py:310
  (18 shorter events, 0.1 us)
Async XLA Ops:
  0.0 0.7 copy-start.7
  0.7 0.7 copy-start.8
  2.7 26.1 %all-to-all-start = ((s32[16,1,128]{2,1,0:T(1,128)}), s32[16,1,128]{2,1,0:T(1,128)S(1)}, u32[]{:S(2)}, u32[]{:S(2)}) async-start(s32[16,1,128]{2,1,0:T(1,128)} %get-tuple-element.14), calls=%async_computation | async-start | bytes 16384 | tf_op jit(solution)/shard_map/all_to_all | solution.py:333
  28.8 1.0 copy-start
  29.8 9.3 %copy-start.12 = (bf16[64,256]{1,0:T(8,128)(2,1)S(1)}, bf16[64,256]{1,0:T(8,128)(2,1)}, u32[]{:S(2)}) copy-start(bf16[64,256]{1,0:T(8,128)(2,1)} %get-tuple-element.17) | copy-start | bytes 98308
  29.8 14.3 %copy-start.1 = (bf16[1024,256]{1,0:T(8,128)(2,1)S(1)}, bf16[1024,256]{1,0:T(8,128)(2,1)}, u32[]{:S(2)}) copy-start(bf16[1024,256]{1,0:T(8,128)(2,1)} %get-tuple-element.15) | copy-start | bytes 1572868
  29.8 17.0 %copy-start.11 = (bf16[64,256]{1,0:T(8,128)(2,1)S(1)}, bf16[64,256]{1,0:T(8,128)(2,1)}, u32[]{:S(2)}) copy-start(bf16[64,256]{1,0:T(8,128)(2,1)} %get-tuple-element.18) | copy-start | bytes 98308
  29.8 48.0 %copy-start.10 = (bf16[16,256]{1,0:T(8,128)(2,1)S(1)}, bf16[16,256]{1,0:T(8,128)(2,1)}, u32[]{:S(2)}) copy-start(bf16[16,256]{1,0:T(8,128)(2,1)} %get-tuple-element.19) | copy-start | bytes 24580
  29.8 51.1 %copy-start.9 = (bf16[16,256]{1,0:T(8,128)(2,1)S(1)}, bf16[16,256]{1,0:T(8,128)(2,1)}, u32[]{:S(2)}) copy-start(bf16[16,256]{1,0:T(8,128)(2,1)} %get-tuple-element.20) | copy-start | bytes 24580
  31.9 71.9 %all-to-all-start.1 = ((bf16[16,2,128,256]{3,2,1,0:T(8,128)(2,1)}), bf16[16,2,128,256]{3,2,1,0:T(8,128)(2,1)S(1)}, u32[]{:S(2)}, u32[]{:S(2)}) async-start(bf16[16,2,128,256]{3,2,1,0:T(8,128)(2,1)} %pack_blocks.1), calls=%async_computation.1 | async-start | bytes 4194304 | tf_op jit(solution)/shard_map/all_to_all | solution.py:340
  39.1 35.9 %collective-permute-start = (bf16[64,256]{1,0:T(8,128)(2,1)S(1)}, bf16[64,256]{1,0:T(8,128)(2,1)S(1)}, u32[]{:S(2)}, u32[]{:S(2)}) collective-permute-start(bf16[64,256]{1,0:T(8,128)(2,1)S(1)} %copy-done.12), channel_id=1, source_target_pairs={{0,8},{8,16},{16,24},{24,32},{32,40},{40,48},{48,56},{56,64},{64,7... | collective-permute-start | bytes 98312 | tf_op jit(solution)/shard_map/ppermute | solution.py:323
  44.2 58.8 %collective-permute-start.4 = (bf16[1024,256]{1,0:T(8,128)(2,1)S(1)}, bf16[1024,256]{1,0:T(8,128)(2,1)S(1)}, u32[]{:S(2)}, u32[]{:S(2)}) collective-permute-start(bf16[1024,256]{1,0:T(8,128)(2,1)S(1)} %copy-done.1), channel_id=1, source_target_pairs={{0,7},{1,6},{2,5},{3,4},{4,3},{5,2},{6,1},{7,0},{8,15},{9,14},{10,... | collective-permute-start | bytes 1572872 | tf_op jit(solution)/shard_map/ppermute | solution.py:341
  46.8 31.0 %collective-permute-start.1 = (bf16[64,256]{1,0:T(8,128)(2,1)S(1)}, bf16[64,256]{1,0:T(8,128)(2,1)S(1)}, u32[]{:S(2)}, u32[]{:S(2)}) collective-permute-start(bf16[64,256]{1,0:T(8,128)(2,1)S(1)} %copy-done.11), channel_id=1, source_target_pairs={{8,0},{16,8},{24,16},{32,24},{40,32},{48,40},{56,48},{64,56},{72,6... | collective-permute-start | bytes 98312 | tf_op jit(solution)/shard_map/ppermute | solution.py:323
  77.8 19.3 %collective-permute-start.2 = (bf16[18,256]{1,0:T(8,128)(2,1)S(1)}, bf16[18,256]{1,0:T(8,128)(2,1)S(1)}, u32[]{:S(2)}, u32[]{:S(2)}) collective-permute-start(bf16[18,256]{1,0:T(8,128)(2,1)S(1)} %pad_maximum_fusion), channel_id=1, source_target_pairs={{0,1},{1,2},{2,3},{3,4},{4,5},{5,6},{6,7},{8,9},{9,10},{10,11},{11... | collective-permute-start | bytes 27656 | tf_op jit(solution)/shard_map/ppermute | solution.py:323
  81.0 16.1 %collective-permute-start.3 = (bf16[18,256]{1,0:T(8,128)(2,1)S(1)}, bf16[18,256]{1,0:T(8,128)(2,1)S(1)}, u32[]{:S(2)}, u32[]{:S(2)}) collective-permute-start(bf16[18,256]{1,0:T(8,128)(2,1)S(1)} %pad_maximum_fusion.1), channel_id=1, source_target_pairs={{1,0},{2,1},{3,2},{4,3},{5,4},{6,5},{7,6},{9,8},{10,9},{11,10},{12... | collective-permute-start | bytes 27656 | tf_op jit(solution)/shard_map/ppermute | solution.py:323
  82.4 14.7 %copy-start.5 = (bf16[256,256]{1,0:T(8,128)(2,1)S(1)}, bf16[256,256]{1,0:T(8,128)(2,1)}, u32[]{:S(2)}) copy-start(bf16[256,256]{1,0:T(8,128)(2,1)} %prop_ref.1) | copy-start | bytes 393220
  82.4 21.3 %copy-start.6 = (s32[16,64]{1,0:T(8,128)S(1)}, s32[16,64]{1,0:T(8,128)}, u32[]{:S(2)}) copy-start(s32[16,64]{1,0:T(8,128)} %mask_ref.1) | copy-start | bytes 12292
  97.1 1.0 copy-start.2
  102.9 0.8 copy-start.3
  103.7 1.0 copy-start.4

commit v3 on v2

v3 whole, which is shorter than its diff:
```python
import functools

import jax
import jax.numpy as jnp
from jax import lax
from jax.experimental import pallas as pl
from jax.experimental.pallas import tpu as pltpu
from jax.sharding import PartitionSpec as P


epsilon = 1e-06
inverse_divisor = 10.0
CAP = 2
LANES = 128
VMEM = pl.BlockSpec(memory_space=pltpu.VMEM)
SMEM = pl.BlockSpec(memory_space=pltpu.SMEM)
ANY = pl.BlockSpec(memory_space=pl.ANY)
LIMIT = 60 * 2**20
SMALL = pltpu.CompilerParams(vmem_limit_bytes=12 * 2**20)
WHOLE = pltpu.CompilerParams(vmem_limit_bytes=LIMIT)
f32 = jnp.float32
bf16 = jnp.bfloat16


def normalize(vector):
    return vector * lax.rsqrt(jnp.sum(vector * vector, axis=-1, keepdims=True) + epsilon)


def transposed_dot(left, right):
    return lax.dot_general(left, right, (((1,), (1,)), ((), ())), preferred_element_type=f32)


def plan_kernel(shard_any, block_any, want_ref, slot_ref, shard_ref, block_ref, sems):
    _, _, per, blocks = shard_ref.shape
    loads = [
        pltpu.make_async_copy(shard_any, shard_ref, sems.at[0]),
        pltpu.make_async_copy(block_any, block_ref, sems.at[1]),
    ]
    for load in loads:
        load.start()
    for load in loads:
        load.wait()
    shards = want_ref.shape[0]
    rows = lax.broadcasted_iota(jnp.int32, (shards, LANES), 0)
    lanes = lax.broadcasted_iota(jnp.int32, (shards, LANES), 1)
    want = jnp.zeros((shards, LANES), jnp.int32)
    chosen = []
    for block in range(blocks):
        for n in range(per):
            shard = shard_ref[0, 0, n, block]
            rank = jnp.int32(0)
            for other in chosen:
                rank = rank + (other == shard).astype(jnp.int32)
            rank = jnp.minimum(rank, CAP - 1)
            chosen.append(shard)
            slot_ref[block * per + n] = shard * CAP + rank
            want = jnp.where((rows == shard) & (lanes == rank), block_ref[0, 0, n, block], want)
    want_ref[...] = want.reshape(want_ref.shape)


def plan_slots(neg_shard, neg_block, shards):
    entries = neg_shard.size
    flipped = [array.transpose(0, 1, 3, 2) for array in (neg_shard, neg_block)]
    return pl.pallas_call(
        plan_kernel,
        in_specs=[ANY, ANY],
        out_specs=[VMEM, SMEM],
        scratch_shapes=[
            pltpu.SMEM(flipped[0].shape, jnp.int32),
            pltpu.SMEM(flipped[1].shape, jnp.int32),
            pltpu.SemaphoreType.DMA((2,)),
        ],
        out_shape=[
            jax.ShapeDtypeStruct((shards, 1, LANES), jnp.int32),
            jax.ShapeDtypeStruct((entries,), jnp.int32),
        ],
        compiler_params=WHOLE,
        name="plan_slots",
    )(*flipped)


PARTS = 4
PIECE = 16


def project_kernel(*refs, columns):
    feat_hbm, hidden_hbm, out_hbm, map_ref = refs[:4]
    edges = refs[4:-5]
    feat, total, hidden_w, out_w, sems = refs[-5:]
    pixels, channels = feat_hbm.shape
    half = pixels // 2
    span = channels // PARTS
    cuts = [slice(part * span, (part + 1) * span) for part in range(PARTS)]

    def copy(source, target, sem):
        return pltpu.make_async_copy(source, target, sems.at[sem])

    feats = [copy(feat_hbm.at[0:half, c], feat.at[0:half, c], i) for i, c in enumerate(cuts)]
    pieces = [copy(hidden_hbm.at[c], hidden_w.at[c], PARTS + i) for i, c in enumerate(cuts)]
    later = [
        copy(out_hbm, out_w, 2 * PARTS),
        copy(feat_hbm.at[half:pixels], feat.at[half:pixels], 2 * PARTS + 1),
    ]
    for first, second in zip(feats, pieces):
        first.start()
        second.start()
    for one in later:
        one.start()
    for part, cut in enumerate(cuts):
        feats[part].wait()
        pieces[part].wait()
        term = jnp.dot(feat[0:half, cut], hidden_w[cut, :], preferred_element_type=f32)
        if part == 0:
            total[...] = term
        elif part < PARTS - 1:
            total[...] += term
        else:
            hidden = jnp.maximum(total[...] + term, 0.0).astype(bf16)
    later[0].wait()
    raw = jnp.dot(hidden, out_w[...], preferred_element_type=f32)
    map_ref[0:half] = normalize(raw).astype(bf16)
    later[1].wait()
    hidden = jnp.dot(feat[half:], hidden_w[...], preferred_element_type=f32)
    hidden = jnp.maximum(hidden, 0.0).astype(bf16)
    raw = jnp.dot(hidden, out_w[...], preferred_element_type=f32)
    map_ref[half:pixels] = normalize(raw).astype(bf16)
    if edges:
        first_row, last_row, first_col, last_col, *corners = edges
        height = first_col.shape[0]
        end = pixels - columns
        first_row[...] = map_ref[0:columns]
        last_row[...] = map_ref[end:pixels]
        row = lax.broadcasted_iota(jnp.int32, (2 * height, pixels), 0)
        place = lax.broadcasted_iota(jnp.int32, (2 * height, pixels), 1)
        wanted = jnp.where(row < height, row * columns, (row - height + 1) * columns - 1)
        pick = (place == wanted).astype(f32).astype(bf16)
        taken = jnp.dot(pick, map_ref[...], preferred_element_type=f32).astype(bf16)
        first_col[...] = taken[0:height]
        last_col[...] = taken[height:]
        begins = (0, columns - PIECE, end, pixels - PIECE)
        for ref, begin in zip(corners, begins):
            ref[...] = map_ref[begin : begin + PIECE]


def project(feat_map, w_hidden, w_out, edges=False):
    height, columns, channels = feat_map.shape
    pixels = height * columns
    hidden, width = w_out.shape
    sizes = (pixels,)
    if edges:
        sizes += (columns, columns, height, height) + (PIECE,) * 4
    results = pl.pallas_call(
        functools.partial(project_kernel, columns=columns),
        in_specs=[ANY] * 3,
        out_specs=[VMEM] * len(sizes),
        out_shape=[jax.ShapeDtypeStruct((size, width), bf16) for size in sizes],
        scratch_shapes=[
            pltpu.VMEM((pixels, channels), bf16),
            pltpu.VMEM((pixels // 2, hidden), f32),
            pltpu.VMEM((channels, hidden), bf16),
            pltpu.VMEM((hidden, width), bf16),
            pltpu.SemaphoreType.DMA((2 * PARTS + 2,)),
        ],
        compiler_params=pltpu.CompilerParams(vmem_limit_bytes=LIMIT),
        cost_estimate=pl.CostEstimate(
            flops=2 * pixels * hidden * (channels + width),
            bytes_accessed=2 * (pixels * channels + hidden * (channels + width)),
            transcendentals=0,
        ),
    )(feat_map.reshape(pixels, channels), w_hidden, w_out)
    return results if edges else results[0]


def pack_kernel(req_ref, keys_any, out_ref, keys_ref, sem, load_sem):
    load = pltpu.make_async_copy(keys_any, keys_ref, load_sem)
    load.start()
    load.wait()
    for shard in range(out_ref.shape[0]):
        for rank in range(CAP):
            source = keys_ref.at[req_ref[shard, 0, rank]]
            pltpu.make_async_copy(source, out_ref.at[shard, rank], sem).start()
    pltpu.make_async_copy(out_ref, out_ref, sem).wait()


def pack(req, key_blocks):
    return pl.pallas_call(
        pack_kernel,
        in_specs=[SMEM, ANY],
        out_specs=ANY,
        out_shape=jax.ShapeDtypeStruct((req.shape[0], CAP) + key_blocks.shape[1:], bf16),
        scratch_shapes=[
            pltpu.VMEM(key_blocks.shape, bf16),
            pltpu.SemaphoreType.DMA,
            pltpu.SemaphoreType.DMA,
        ],
        compiler_params=WHOLE,
        name="pack_blocks",
    )(req, key_blocks)


def split(value):
    high = value.astype(bf16)
    return high, (value - high.astype(f32)).astype(bf16)


def weights(dots, keep):
    value = jnp.maximum(dots, 0.0)
    return split(jnp.where(keep, value * value, 0.0))


def weighted(pair, high, low):
    top, rest = pair
    return (
        jnp.dot(top, high, preferred_element_type=f32)
        + jnp.dot(top, low, preferred_element_type=f32)
        + jnp.dot(rest, high, preferred_element_type=f32)
    )


def spread_kernel(own_any, prop_ref, out_ref, same_ref, rows_ref, high_ref, low_ref, sem, *, columns):
    pixels, width = out_ref.shape
    end = columns + pixels
    load = pltpu.make_async_copy(own_any, rows_ref.at[columns:end], sem)
    load.start()
    rows_ref[0:columns] = jnp.zeros((columns, width), bf16)
    rows_ref[end:] = jnp.zeros((columns, width), bf16)
    size = 2 * columns
    reach = 4 * columns
    pix = lax.broadcasted_iota(jnp.int32, (size, reach), 0)
    oth = lax.broadcasted_iota(jnp.int32, (size, reach), 1)
    apart = oth // columns - pix // columns
    across = oth % columns - pix % columns
    near = (apart >= 0) & (apart <= 2) & (across >= -1) & (across <= 1)
    load.wait()
    carried = jnp.dot(rows_ref[...], prop_ref[...], preferred_element_type=f32)
    high_ref[...], low_ref[...] = split(carried)
    for block in range(pixels // size):
        base = block * size
        around = slice(base, base + reach)
        own = rows_ref[base + columns : base + columns + size]
        main = weights(transposed_dot(own, rows_ref[around]), near)
        same_ref[base : base + size] = own
        out_ref[base : base + size] = weighted(main, high_ref[around], low_ref[around])


def propagate(own, w_prop, columns):
    pixels, width = own.shape
    total = pixels + 2 * columns
    return pl.pallas_call(
        functools.partial(spread_kernel, columns=columns),
        in_specs=[ANY, VMEM],
        out_specs=[VMEM, VMEM],
        out_shape=[
            jax.ShapeDtypeStruct((pixels, width), f32),
            jax.ShapeDtypeStruct((pixels, width), bf16),
        ],
        scratch_shapes=[
            pltpu.VMEM((total, width), bf16),
            pltpu.VMEM((total, width), bf16),
            pltpu.VMEM((total, width), bf16),
            pltpu.SemaphoreType.DMA,
        ],
        compiler_params=SMALL,
        cost_estimate=pl.CostEstimate(
            flops=2 * 10**9, bytes_accessed=2 * 10**6, transcendentals=0
        ),
        name="propagate",
    )(own, w_prop)


def loss_kernel(
    slot_ref,
    own_ref,
    spread_ref,
    top_ref,
    bottom_ref,
    left_ref,
    right_ref,
    above_left,
    above_right,
    below_left,
    below_right,
    prop_ref,
    keys_ref,
    partner_ref,
    mask_ref,
    out_ref,
    halo_ref,
    high_ref,
    low_ref,
    query_ref,
):
    height, columns = out_ref.shape
    pixels, _ = own_ref.shape
    size = 2 * columns
    blocks = pixels // size
    per = slot_ref.shape[0] // blocks
    start = 2 * columns
    halo_ref[0:columns] = top_ref[...]
    halo_ref[columns:start] = bottom_ref[...]
    place = start
    for ref in (left_ref, right_ref, above_left, above_right, below_left, below_right):
        halo_ref[place : place + ref.shape[0]] = ref[...]
        place += ref.shape[0]
    carried = jnp.dot(halo_ref[...], prop_ref[...], preferred_element_type=f32)
    high_ref[...], low_ref[...] = split(carried)

    here = lax.broadcasted_iota(jnp.int32, (size, size), 0)
    there = lax.broadcasted_iota(jnp.int32, (size, size), 1)
    mirrored = (here // columns == there // columns) & (
        here % columns + there % columns == columns - 1
    )
    pix = lax.broadcasted_iota(jnp.int32, (size, columns), 0)
    oth = lax.broadcasted_iota(jnp.int32, (size, columns), 1)
    across = oth - pix % columns
    level = (across >= -1) & (across <= 1)
    side = place - start
    spix = lax.broadcasted_iota(jnp.int32, (size, side), 0)
    soth = lax.broadcasted_iota(jnp.int32, (size, side), 1)
    far = -4 * pixels
    srow = jnp.where(soth < height, soth, soth - height)
    scol = jnp.where(soth < height, -1, columns)
    lone = soth - 2 * height
    corners = ((PIECE - 1, -1, -1), (0, -1, columns), (PIECE - 1, height, -1), (0, height, columns))
    srow = jnp.where(lone >= 0, far, srow)
    for group, (offset, row, col) in enumerate(corners):
        here_it_is = lone == group * PIECE + offset
        srow = jnp.where(here_it_is, row, srow)
        scol = jnp.where(here_it_is, col, scol)
    srow = srow - spix // columns
    scol = scol - spix % columns
    edge = (scol >= -1) & (scol <= 1)

    for block in range(blocks):
        at = slice(block * size, (block + 1) * size)
        own = own_ref[at]
        spread = spread_ref[at]
        cuts = [(slice(start, place), None)]
        if block == 0:
            cuts.append((slice(0, columns), 0))
        if block == blocks - 1:
            cuts.append((slice(columns, start), 1))
        for cut, row in cuts:
            if row is None:
                keep = edge & (srow >= 2 * block - 1) & (srow <= 2 * block + 1)
            else:
                keep = level & (pix // columns == row)
            pair = weights(transposed_dot(own, halo_ref[cut]), keep)
            spread = spread + weighted(pair, high_ref[cut], low_ref[cut])
        query_ref[at] = normalize(spread).astype(bf16)
    for block in range(blocks):
        at = slice(block * size, (block + 1) * size)
        query = query_ref[at]
        match = transposed_dot(partner_ref[at], query)
        match = jnp.sum(jnp.where(mirrored, match, 0.0), axis=0, keepdims=True)
        positive = match * inverse_divisor
        total = jnp.exp(positive)
        for n in range(per):
            keys = keys_ref[slot_ref[block * per + n]]
            logits = transposed_dot(keys, query) * inverse_divisor
            total = total + jnp.sum(jnp.exp(logits), axis=0, keepdims=True)
        loss = jnp.log(total) - positive
        for row in range(2):
            line = slice(2 * block + row, 2 * block + row + 1)
            piece = loss[:, row * columns : (row + 1) * columns]
            out_ref[line, :] = mask_ref[line, :].astype(f32) * piece


def loss_of(slot, own, spread, halos, w_prop, received, partner, mask):
    width = own.shape[1]
    total = sum(halo.shape[0] for halo in halos)
    return pl.pallas_call(
        loss_kernel,
        in_specs=[SMEM] + [VMEM] * 14,
        out_specs=VMEM,
        out_shape=jax.ShapeDtypeStruct(mask.shape, f32),
        scratch_shapes=[pltpu.VMEM((total, width), bf16)] * 3 + [pltpu.VMEM(own.shape, bf16)],
        compiler_params=SMALL,
        name="loss_blocks",
    )(slot, own, spread, *halos, w_prop, received, partner, mask)


def moved(value, down, across):
    rows, cols = lax.axis_size("rows"), lax.axis_size("cols")
    pairs = []
    for row in range(rows):
        for col in range(cols):
            if 0 <= row + down < rows and 0 <= col + across < cols:
                pairs.append((row * cols + col, (row + down) * cols + col + across))
    return lax.ppermute(value, ("rows", "cols"), pairs)


def per_device(feat_query, feat_key, w_hidden, w_out, w_prop, valid_mask, neg_shard, neg_block):
    height, columns, _ = feat_query.shape
    pixels = height * columns
    per_tile = pixels // 128
    shards = lax.axis_size("rows")
    cols = lax.axis_size("cols")
    want, slot = plan_slots(neg_shard, neg_block, shards)
    req = lax.all_to_all(want, "rows", 0, 0, tiled=True)
    key_map = project(feat_key, w_hidden, w_out)
    width = key_map.shape[-1]
    partner = lax.ppermute(key_map, "cols", [(i, cols - 1 - i) for i in range(cols)])
    send = pack(req, key_map.reshape(per_tile, 128, width))
    received = lax.all_to_all(send, "rows", 0, 0, tiled=True)
    received = received.reshape(shards * CAP, 128, width)
    feat_query, _ = lax.optimization_barrier((feat_query, send))
    query, *edges = project(feat_query, w_hidden, w_out, True)
    first_row, last_row, first_col, last_col, *corners = edges
    steps = (
        (last_row, 1, 0),
        (first_row, -1, 0),
        (last_col, 0, 1),
        (first_col, 0, -1),
        (corners[3], 1, 1),
        (corners[2], 1, -1),
        (corners[1], -1, 1),
        (corners[0], -1, -1),
    )
    halos = [moved(value, down, across) for value, down, across in steps]
    spread, own = propagate(query, w_prop, columns)
    return loss_of(slot, own, spread, halos, w_prop, received, partner, valid_mask)


def solution(mesh):
    in_specs = (
        P("rows", "cols", None),
        P("rows", "cols", None),
        P(),
        P(),
        P(),
        P("rows", "cols"),
        P("rows", "cols", None, None),
        P("rows", "cols", None, None),
    )
    out_specs = P("rows", "cols")
    return jax.shard_map(
        per_device, mesh=mesh, in_specs=in_specs, out_specs=out_specs, check_vma=False
    )
```

time: 108 us -> 96.8 us (0.90)
  the two profiles are of different devices: /device:TPU:1 before, /device:TPU:27 now
where the time goes in v3:
time: 96.8 us; the launch traced here: 96.1 us
  starting transfers between devices  42.3 us (44%)
  Pallas kernels  38.5 us (40%)
  waiting for transfers between devices  9.77 us (10%)
  local copies, waits for them, and re-layouts  5.31 us (5%)
    pallas_call x2, Pallas kernels, project(): pl.pallas_call(functools.partial(project_kernel, columns=columns), in_spe...  29.3 us
    ppermute x8, starting transfers between devices, moved(): return lax.ppermute(value, ('rows', 'cols'), pairs)  25.1 us
    ppermute x8, waiting for transfers between devices, moved(): return lax.ppermute(value, ('rows', 'cols'), pairs)  9.77 us
    all_to_all x1, starting transfers between devices, per_device(): req = lax.all_to_all(want, 'rows', 0, 0, tiled=True)  8.59 us
    all_to_all x1, starting transfers between devices, per_device(): received = lax.all_to_all(send, 'rows', 0, 0, tiled=True)  7.24 us
    unnamed x18, local copies, waits for them, and re-layouts  5.31 us
    pallas_call x1, Pallas kernels, pack(): pl.pallas_call(pack_kernel, in_specs=[SMEM, ANY], out_specs=ANY, out_shap...  3.18 us
    pallas_call x1, Pallas kernels, loss_of(): pl.pallas_call(loss_kernel, in_specs=[SMEM] + [VMEM] * 14, out_specs=VMEM...  3.01 us
  transfers between devices with their start and end apart: 11, of which 2 were waited for; matrix products, arithmetic and copies ran while one was open for 0% of the time, Pallas kernels for 32%

profile of v3, /device:TPU:27, one launch (start us, length us, event | category | flops | bytes accessed | tf_op | source)
XLA Modules:
  0.0 96.1 jit_solution(15768274895626446447)
XLA Ops:
  0.0 1.5 %plan_slots.1 = (s32[16,1,128]{2,1,0:T(1,128)}, s32[16]{0:T(128)}) custom-call(s32[1,1,2,8]{3,2,1,0:T(2,128)} %bitcast.7, s32[1,1,2,8]{3,2,1,0:T(2,128)} %bitcast.8), custom_call_target="tpu_custom_call" | custom-call | tf_op jit(solution)/shard_map/plan_slots/pallas_call | solution.py:64
  1.5 8.6 %all-to-all-start = ((s32[16,1,128]{2,1,0:T(1,128)}), s32[16,1,128]{2,1,0:T(1,128)S(1)}, u32[]{:S(2)}, u32[]{:S(2)}) async-start(s32[16,1,128]{2,1,0:T(1,128)} %get-tuple-element.20), calls=%async_computation | async-start | bytes 16384 | tf_op jit(solution)/shard_map/all_to_all | solution.py:400
  10.1 14.6 %shard_map.82 = bf16[1024,256]{1,0:T(8,128)(2,1)} custom-call(bf16[1024,2048]{1,0:T(8,128)(2,1)} %bitcast.9, bf16[2048,2048]{1,0:T(8,128)(2,1)} %refs_1_.3, bf16[2048,256]{1,0:T(8,128)(2,1)} %refs_2_.3), custom_call_target="tpu_custom_call" | custom-call | flops 9663676416 | bytes 13631488 | tf_op jit(solution)/shard_map/pallas_call | solution.py:152
  24.6 0.0 all-to-all-done.req_ref
  24.7 0.0 copy-start.8
  24.7 0.6 copy-done.8
  25.3 3.2 %pack_blocks.1 = bf16[16,2,128,256]{3,2,1,0:T(8,128)(2,1)} custom-call(s32[16,1,128]{2,1,0:T(1,128)} %copy-done.8, bf16[8,128,256]{2,1,0:T(8,128)(2,1)} %bitcast.3.keys_any), custom_call_target="tpu_custom_call" | custom-call | tf_op jit(solution)/shard_map/pack_blocks/pallas_call | solution.py:186
  28.5 7.2 %all-to-all-start.1 = ((bf16[16,2,128,256]{3,2,1,0:T(8,128)(2,1)}), bf16[16,2,128,256]{3,2,1,0:T(8,128)(2,1)S(1)}, u32[]{:S(2)}, u32[]{:S(2)}) async-start(bf16[16,2,128,256]{3,2,1,0:T(8,128)(2,1)} %pack_blocks.1), calls=%async_computation.1 | async-start | bytes 4194304 | tf_op jit(solution)/shard_map/all_to_all | solution.py:405
  35.7 1.4 %collective-permute-start.8 = (bf16[1024,256]{1,0:T(8,128)(2,1)}, bf16[1024,256]{1,0:T(8,128)(2,1)S(1)}, u32[]{:S(2)}, u32[]{:S(2)}) collective-permute-start(bf16[1024,256]{1,0:T(8,128)(2,1)} %shard_map.82), channel_id=1, source_target_pairs={{0,7},{1,6},{2,5},{3,4},{4,3},{5,2},{6,1},{7,0},{8,15},{9,14},{10,... | collective-permute-start | bytes 1572872 | tf_op jit(solution)/shard_map/ppermute | solution.py:403
  37.1 14.7 %shard_map.83 = (bf16[1024,256]{1,0:T(8,128)(2,1)}, bf16[64,256]{1,0:T(8,128)(2,1)}, bf16[64,256]{1,0:T(8,128)(2,1)}, bf16[16,256]{1,0:T(8,128)(2,1)}, bf16[16,2...) custom-call(bf16[1024,2048]{1,0:T(8,128)(2,1)} %bitcast.10, ...), custom_call_target="tpu_custom_call" | custom-call | flops 9663676416 | bytes 13631488 | tf_op jit(solution)/shard_map/pallas_call | solution.py:152
  51.8 0.0 copy-start.5
  51.8 2.9 %collective-permute-start.2 = (bf16[16,256]{1,0:T(8,128)(2,1)}, bf16[16,256]{1,0:T(8,128)(2,1)S(1)}, u32[]{:S(2)}, u32[]{:S(2)}) collective-permute-start(bf16[16,256]{1,0:T(8,128)(2,1)} %get-tuple-element.27), channel_id=1, source_target_pairs={{0,1},{1,2},{2,3},{3,4},{4,5},{5,6},{6,7},{8,9},{9,10},{10,11},{11... | collective-permute-start | bytes 24584 | tf_op jit(solution)/shard_map/ppermute | solution.py:390
  54.7 2.4 %collective-permute-start.3 = (bf16[16,256]{1,0:T(8,128)(2,1)}, bf16[16,256]{1,0:T(8,128)(2,1)S(1)}, u32[]{:S(2)}, u32[]{:S(2)}) collective-permute-start(bf16[16,256]{1,0:T(8,128)(2,1)} %get-tuple-element.28), channel_id=1, source_target_pairs={{1,0},{2,1},{3,2},{4,3},{5,4},{6,5},{7,6},{9,8},{10,9},{11,10},{12... | collective-permute-start | bytes 24584 | tf_op jit(solution)/shard_map/ppermute | solution.py:390
  57.1 4.9 %collective-permute-start.4 = (bf16[16,256]{1,0:T(8,128)(2,1)}, bf16[16,256]{1,0:T(8,128)(2,1)S(1)}, u32[]{:S(2)}, u32[]{:S(2)}) collective-permute-start(bf16[16,256]{1,0:T(8,128)(2,1)} %get-tuple-element.29), channel_id=1, source_target_pairs={{0,9},{1,10},{2,11},{3,12},{4,13},{5,14},{6,15},{8,17},{9,18},{10,... | collective-permute-start | bytes 24584 | tf_op jit(solution)/shard_map/ppermute | solution.py:390
  62.0 2.0 %collective-permute-start.5 = (bf16[16,256]{1,0:T(8,128)(2,1)}, bf16[16,256]{1,0:T(8,128)(2,1)S(1)}, u32[]{:S(2)}, u32[]{:S(2)}) collective-permute-start(bf16[16,256]{1,0:T(8,128)(2,1)} %get-tuple-element.30), channel_id=1, source_target_pairs={{1,8},{2,9},{3,10},{4,11},{5,12},{6,13},{7,14},{9,16},{10,17},{11,... | collective-permute-start | bytes 24584 | tf_op jit(solution)/shard_map/ppermute | solution.py:390
  64.0 7.3 %collective-permute-done.2.left_ref = bf16[16,256]{1,0:T(8,128)(2,1)S(1)} collective-permute-done((bf16[16,256]{1,0:T(8,128)(2,1)}, bf16[16,256]{1,0:T(8,128)(2,1)S(1)}, u32[]{:S(2)}, u32[]{:S(2)}) %collective-permute-start.2) | collective-permute-done | bytes 8224 | tf_op jit(solution)/shard_map/ppermute | solution.py:390
  71.3 3.0 %collective-permute-start.6 = (bf16[16,256]{1,0:T(8,128)(2,1)}, bf16[16,256]{1,0:T(8,128)(2,1)S(1)}, u32[]{:S(2)}, u32[]{:S(2)}) collective-permute-start(bf16[16,256]{1,0:T(8,128)(2,1)} %get-tuple-element.31), channel_id=1, source_target_pairs={{8,1},{9,2},{10,3},{11,4},{12,5},{13,6},{14,7},{16,9},{17,10},{18,... | collective-permute-start | bytes 24584 | tf_op jit(solution)/shard_map/ppermute | solution.py:390
  74.3 2.6 %collective-permute-start.7 = (bf16[16,256]{1,0:T(8,128)(2,1)}, bf16[16,256]{1,0:T(8,128)(2,1)S(1)}, u32[]{:S(2)}, u32[]{:S(2)}) collective-permute-start(bf16[16,256]{1,0:T(8,128)(2,1)} %get-tuple-element.32), channel_id=1, source_target_pairs={{9,0},{10,1},{11,2},{12,3},{13,4},{14,5},{15,6},{17,8},{18,9},{19,... | collective-permute-start | bytes 24584 | tf_op jit(solution)/shard_map/ppermute | solution.py:390
  76.9 5.4 %collective-permute-start = (bf16[64,256]{1,0:T(8,128)(2,1)}, bf16[64,256]{1,0:T(8,128)(2,1)S(1)}, u32[]{:S(2)}, u32[]{:S(2)}) collective-permute-start(bf16[64,256]{1,0:T(8,128)(2,1)} %get-tuple-element.25), channel_id=1, source_target_pairs={{0,8},{1,9},{2,10},{3,11},{4,12},{5,13},{6,14},{7,15},{8,16},{9,17... | collective-permute-start | bytes 98312 | tf_op jit(solution)/shard_map/ppermute | solution.py:390
  82.3 1.9 %collective-permute-start.1 = (bf16[64,256]{1,0:T(8,128)(2,1)}, bf16[64,256]{1,0:T(8,128)(2,1)S(1)}, u32[]{:S(2)}, u32[]{:S(2)}) collective-permute-start(bf16[64,256]{1,0:T(8,128)(2,1)} %get-tuple-element.26), channel_id=1, source_target_pairs={{8,0},{9,1},{10,2},{11,3},{12,4},{13,5},{14,6},{15,7},{16,8},{17,9... | collective-permute-start | bytes 98312 | tf_op jit(solution)/shard_map/ppermute | solution.py:390
  84.3 1.0 %copy-done.7 = bf16[1024,256]{1,0:T(8,128)(2,1)S(1)} copy-done((bf16[1024,256]{1,0:T(8,128)(2,1)S(1)}, bf16[1024,256]{1,0:T(8,128)(2,1)}, u32[]{:S(2)}) %copy-start.7) | copy-done | bytes 524312
  85.3 1.6 %propagate.1 = (f32[1024,256]{1,0:T(8,128)S(1)}, bf16[1024,256]{1,0:T(8,128)(2,1)S(1)}) custom-call(bf16[1024,256]{1,0:T(8,128)(2,1)S(1)} %copy-done.7, bf16[256,256]{1,0:T(8,128)(2,1)S(1)} %copy-done.4), custom_call_target="tpu_custom_call" | custom-call | flops 2000000000 | bytes 2000000 | tf_op jit(solution)/shard_map/propagate/pallas_call | solution.py:249
  87.0 0.8 copy-done.2
  87.7 0.0 collective-permute-done.6.below_left
  87.7 0.0 collective-permute-done.7.below_right
  87.8 0.0 collective-permute-done.top_ref
  87.8 2.4 %collective-permute-done.1.bottom_ref = bf16[64,256]{1,0:T(8,128)(2,1)S(1)} collective-permute-done((bf16[64,256]{1,0:T(8,128)(2,1)}, bf16[64,256]{1,0:T(8,128)(2,1)S(1)}, u32[]{:S(2)}, u32[]{:S(2)}) %collective-permute-start.1) | collective-permute-done | bytes 32800 | tf_op jit(solution)/shard_map/ppermute | solution.py:390
  90.2 0.0 collective-permute-done.8.partner_ref
  90.2 0.8 copy-done
  91.0 1.0 %copy-done.1 = bf16[1024,256]{1,0:T(8,128)(2,1)S(1)} copy-done((bf16[1024,256]{1,0:T(8,128)(2,1)S(1)}, bf16[1024,256]{1,0:T(8,128)(2,1)}, u32[]{:S(2)}) %copy-start.1) | copy-done | bytes 524312
  92.1 1.0 %copy-done.3 = bf16[1024,256]{1,0:T(8,128)(2,1)S(1)} copy-done((bf16[1024,256]{1,0:T(8,128)(2,1)S(1)}, bf16[1024,256]{1,0:T(8,128)(2,1)}, u32[]{:S(2)}) %copy-start.3) | copy-done | bytes 524312
  93.1 3.0 %loss_blocks.1 = f32[16,64]{1,0:T(8,128)} custom-call(s32[16]{0:T(128)S(1)} %copy-done.6, bf16[1024,256]{1,0:T(8,128)(2,1)S(1)} %copy-done.3, f32[1024,256]{1,0:T(8,128)S(1)} %get-tuple-element.24.spread_ref, bf16[64,256]{1,0:T(8,128)(2,1)S(1)} %collective-permute-done.top_ref, bf16[64,256]{1,0:T(8,128)(2,1)S(1)} %collective-permute-done.1.bottom_ref, ...), custom_call_target="tpu_custom_call" | custom-call | tf_op jit(solution)/shard_map/loss_blocks/pallas_call | solution.py:372
  (14 shorter events, 0.0 us)
Async XLA Ops:
  1.5 23.2 %all-to-all-start = ((s32[16,1,128]{2,1,0:T(1,128)}), s32[16,1,128]{2,1,0:T(1,128)S(1)}, u32[]{:S(2)}, u32[]{:S(2)}) async-start(s32[16,1,128]{2,1,0:T(1,128)} %get-tuple-element.20), calls=%async_computation | async-start | bytes 16384 | tf_op jit(solution)/shard_map/all_to_all | solution.py:400
  24.7 0.6 copy-start.8
  28.5 62.5 %all-to-all-start.1 = ((bf16[16,2,128,256]{3,2,1,0:T(8,128)(2,1)}), bf16[16,2,128,256]{3,2,1,0:T(8,128)(2,1)S(1)}, u32[]{:S(2)}, u32[]{:S(2)}) async-start(bf16[16,2,128,256]{3,2,1,0:T(8,128)(2,1)} %pack_blocks.1), calls=%async_computation.1 | async-start | bytes 4194304 | tf_op jit(solution)/shard_map/all_to_all | solution.py:405
  35.7 54.5 %collective-permute-start.8 = (bf16[1024,256]{1,0:T(8,128)(2,1)}, bf16[1024,256]{1,0:T(8,128)(2,1)S(1)}, u32[]{:S(2)}, u32[]{:S(2)}) collective-permute-start(bf16[1024,256]{1,0:T(8,128)(2,1)} %shard_map.82), channel_id=1, source_target_pairs={{0,7},{1,6},{2,5},{3,4},{4,3},{5,2},{6,1},{7,0},{8,15},{9,14},{10,... | collective-permute-start | bytes 1572872 | tf_op jit(solution)/shard_map/ppermute | solution.py:403
  37.1 47.2 %copy-start.4 = (bf16[256,256]{1,0:T(8,128)(2,1)S(1)}, bf16[256,256]{1,0:T(8,128)(2,1)}, u32[]{:S(2)}) copy-start(bf16[256,256]{1,0:T(8,128)(2,1)} %prop_ref.3) | copy-start | bytes 393220
  51.8 39.2 %copy-start.5 = (s32[16,64]{1,0:T(8,128)S(1)}, s32[16,64]{1,0:T(8,128)}, u32[]{:S(2)}) copy-start(s32[16,64]{1,0:T(8,128)} %mask_ref.1) | copy-start | bytes 12292
  51.8 39.2 %copy-start.6 = (s32[16]{0:T(128)S(1)}, s32[16]{0:T(128)}, u32[]{:S(2)}) copy-start(s32[16]{0:T(128)} %get-tuple-element.19.slot_ref) | copy-start | bytes 196
  51.8 19.5 %collective-permute-start.2 = (bf16[16,256]{1,0:T(8,128)(2,1)}, bf16[16,256]{1,0:T(8,128)(2,1)S(1)}, u32[]{:S(2)}, u32[]{:S(2)}) collective-permute-start(bf16[16,256]{1,0:T(8,128)(2,1)} %get-tuple-element.27), channel_id=1, source_target_pairs={{0,1},{1,2},{2,3},{3,4},{4,5},{5,6},{6,7},{8,9},{9,10},{10,11},{11... | collective-permute-start | bytes 24584 | tf_op jit(solution)/shard_map/ppermute | solution.py:390
  54.7 19.6 %collective-permute-start.3 = (bf16[16,256]{1,0:T(8,128)(2,1)}, bf16[16,256]{1,0:T(8,128)(2,1)S(1)}, u32[]{:S(2)}, u32[]{:S(2)}) collective-permute-start(bf16[16,256]{1,0:T(8,128)(2,1)} %get-tuple-element.28), channel_id=1, source_target_pairs={{1,0},{2,1},{3,2},{4,3},{5,4},{6,5},{7,6},{9,8},{10,9},{11,10},{12... | collective-permute-start | bytes 24584 | tf_op jit(solution)/shard_map/ppermute | solution.py:390
  57.1 19.8 %collective-permute-start.4 = (bf16[16,256]{1,0:T(8,128)(2,1)}, bf16[16,256]{1,0:T(8,128)(2,1)S(1)}, u32[]{:S(2)}, u32[]{:S(2)}) collective-permute-start(bf16[16,256]{1,0:T(8,128)(2,1)} %get-tuple-element.29), channel_id=1, source_target_pairs={{0,9},{1,10},{2,11},{3,12},{4,13},{5,14},{6,15},{8,17},{9,18},{10,... | collective-permute-start | bytes 24584 | tf_op jit(solution)/shard_map/ppermute | solution.py:390
  62.0 20.3 %collective-permute-start.5 = (bf16[16,256]{1,0:T(8,128)(2,1)}, bf16[16,256]{1,0:T(8,128)(2,1)S(1)}, u32[]{:S(2)}, u32[]{:S(2)}) collective-permute-start(bf16[16,256]{1,0:T(8,128)(2,1)} %get-tuple-element.30), channel_id=1, source_target_pairs={{1,8},{2,9},{3,10},{4,11},{5,12},{6,13},{7,14},{9,16},{10,17},{11,... | collective-permute-start | bytes 24584 | tf_op jit(solution)/shard_map/ppermute | solution.py:390
  71.3 16.5 %collective-permute-start.6 = (bf16[16,256]{1,0:T(8,128)(2,1)}, bf16[16,256]{1,0:T(8,128)(2,1)S(1)}, u32[]{:S(2)}, u32[]{:S(2)}) collective-permute-start(bf16[16,256]{1,0:T(8,128)(2,1)} %get-tuple-element.31), channel_id=1, source_target_pairs={{8,1},{9,2},{10,3},{11,4},{12,5},{13,6},{14,7},{16,9},{17,10},{18,... | collective-permute-start | bytes 24584 | tf_op jit(solution)/shard_map/ppermute | solution.py:390
  74.3 13.5 %collective-permute-start.7 = (bf16[16,256]{1,0:T(8,128)(2,1)}, bf16[16,256]{1,0:T(8,128)(2,1)S(1)}, u32[]{:S(2)}, u32[]{:S(2)}) collective-permute-start(bf16[16,256]{1,0:T(8,128)(2,1)} %get-tuple-element.32), channel_id=1, source_target_pairs={{9,0},{10,1},{11,2},{12,3},{13,4},{14,5},{15,6},{17,8},{18,9},{19,... | collective-permute-start | bytes 24584 | tf_op jit(solution)/shard_map/ppermute | solution.py:390
  76.9 10.9 %collective-permute-start = (bf16[64,256]{1,0:T(8,128)(2,1)}, bf16[64,256]{1,0:T(8,128)(2,1)S(1)}, u32[]{:S(2)}, u32[]{:S(2)}) collective-permute-start(bf16[64,256]{1,0:T(8,128)(2,1)} %get-tuple-element.25), channel_id=1, source_target_pairs={{0,8},{1,9},{2,10},{3,11},{4,12},{5,13},{6,14},{7,15},{8,16},{9,17... | collective-permute-start | bytes 98312 | tf_op jit(solution)/shard_map/ppermute | solution.py:390
  82.3 7.8 %collective-permute-start.1 = (bf16[64,256]{1,0:T(8,128)(2,1)}, bf16[64,256]{1,0:T(8,128)(2,1)S(1)}, u32[]{:S(2)}, u32[]{:S(2)}) collective-permute-start(bf16[64,256]{1,0:T(8,128)(2,1)} %get-tuple-element.26), channel_id=1, source_target_pairs={{8,0},{9,1},{10,2},{11,3},{12,4},{13,5},{14,6},{15,7},{16,8},{17,9... | collective-permute-start | bytes 98312 | tf_op jit(solution)/shard_map/ppermute | solution.py:390
  84.3 1.0 %copy-start.7 = (bf16[1024,256]{1,0:T(8,128)(2,1)S(1)}, bf16[1024,256]{1,0:T(8,128)(2,1)}, u32[]{:S(2)}) copy-start(bf16[1024,256]{1,0:T(8,128)(2,1)} %get-tuple-element.22.own_any) | copy-start | bytes 1572868
  86.9 0.8 copy-start.2
  90.2 0.8 copy-start
  91.0 1.0 %copy-start.1 = (bf16[1024,256]{1,0:T(8,128)(2,1)S(1)}, bf16[1024,256]{1,0:T(8,128)(2,1)}, u32[]{:S(2)}) copy-start(bf16[1024,256]{1,0:T(8,128)(2,1)} %copy-done) | copy-start | bytes 1572868
  92.1 1.0 %copy-start.3 = (bf16[1024,256]{1,0:T(8,128)(2,1)S(1)}, bf16[1024,256]{1,0:T(8,128)(2,1)}, u32[]{:S(2)}) copy-start(bf16[1024,256]{1,0:T(8,128)(2,1)} %copy-done.2) | copy-start | bytes 1572868

commit v4 on v3

--- a/solution.py
+++ b/solution.py
@@ -80,7 +80,6 @@
 
 
 PARTS = 4
-PIECE = 16
 
 
 def project_kernel(*refs, columns):
@@ -125,7 +124,7 @@
     raw = jnp.dot(hidden, out_w[...], preferred_element_type=f32)
     map_ref[half:pixels] = normalize(raw).astype(bf16)
     if edges:
-        first_row, last_row, first_col, last_col, *corners = edges
+        first_row, last_row, first_col, last_col = edges
         height = first_col.shape[0]
         end = pixels - columns
         first_row[...] = map_ref[0:columns]
@@ -137,9 +136,6 @@
         taken = jnp.dot(pick, map_ref[...], preferred_element_type=f32).astype(bf16)
         first_col[...] = taken[0:height]
         last_col[...] = taken[height:]
-        begins = (0, columns - PIECE, end, pixels - PIECE)
-        for ref, begin in zip(corners, begins):
-            ref[...] = map_ref[begin : begin + PIECE]
 
 
 def project(feat_map, w_hidden, w_out, edges=False):
@@ -148,7 +144,7 @@
     hidden, width = w_out.shape
     sizes = (pixels,)
     if edges:
-        sizes += (columns, columns, height, height) + (PIECE,) * 4
+        sizes += (columns, columns, height, height)
     results = pl.pallas_call(
         functools.partial(project_kernel, columns=columns),
         in_specs=[ANY] * 3,
@@ -171,10 +167,7 @@
     return results if edges else results[0]
 
 
-def pack_kernel(req_ref, keys_any, out_ref, keys_ref, sem, load_sem):
-    load = pltpu.make_async_copy(keys_any, keys_ref, load_sem)
-    load.start()
-    load.wait()
+def pack_kernel(req_ref, keys_ref, out_ref, sem):
     for shard in range(out_ref.shape[0]):
         for rank in range(CAP):
             source = keys_ref.at[req_ref[shard, 0, rank]]
@@ -185,15 +178,11 @@
 def pack(req, key_blocks):
     return pl.pallas_call(
         pack_kernel,
-        in_specs=[SMEM, ANY],
+        in_specs=[SMEM, VMEM],
         out_specs=ANY,
         out_shape=jax.ShapeDtypeStruct((req.shape[0], CAP) + key_blocks.shape[1:], bf16),
-        scratch_shapes=[
-            pltpu.VMEM(key_blocks.shape, bf16),
-            pltpu.SemaphoreType.DMA,
-            pltpu.SemaphoreType.DMA,
-        ],
-        compiler_params=WHOLE,
+        scratch_shapes=[pltpu.SemaphoreType.DMA],
+        compiler_params=SMALL,
         name="pack_blocks",
     )(req, key_blocks)
 
@@ -217,7 +206,7 @@
     )
 
 
-def spread_kernel(own_any, prop_ref, out_ref, same_ref, rows_ref, high_ref, low_ref, sem, *, columns):
+def spread_kernel(own_any, prop_ref, out_ref, rows_ref, high_ref, low_ref, sem, *, columns):
     pixels, width = out_ref.shape
     end = columns + pixels
     load = pltpu.make_async_copy(own_any, rows_ref.at[columns:end], sem)
@@ -239,7 +228,6 @@
         around = slice(base, base + reach)
         own = rows_ref[base + columns : base + columns + size]
         main = weights(transposed_dot(own, rows_ref[around]), near)
-        same_ref[base : base + size] = own
         out_ref[base : base + size] = weighted(main, high_ref[around], low_ref[around])
 
 
@@ -249,11 +237,8 @@
     return pl.pallas_call(
         functools.partial(spread_kernel, columns=columns),
         in_specs=[ANY, VMEM],
-        out_specs=[VMEM, VMEM],
-        out_shape=[
-            jax.ShapeDtypeStruct((pixels, width), f32),
-            jax.ShapeDtypeStruct((pixels, width), bf16),
-        ],
+        out_specs=VMEM,
+        out_shape=jax.ShapeDtypeStruct((pixels, width), f32),
         scratch_shapes=[
             pltpu.VMEM((total, width), bf16),
             pltpu.VMEM((total, width), bf16),
@@ -268,18 +253,22 @@
     )(own, w_prop)
 
 
+def outside(own, halo_ref, high_ref, low_ref, cut, keep):
+    pair = weights(transposed_dot(own, halo_ref[cut]), keep)
+    return weighted(pair, high_ref[cut], low_ref[cut])
+
+
 def loss_kernel(
     slot_ref,
-    own_ref,
     spread_ref,
+    first_row,
+    last_row,
+    first_col,
+    last_col,
     top_ref,
     bottom_ref,
     left_ref,
     right_ref,
-    above_left,
-    above_right,
-    below_left,
-    below_right,
     prop_ref,
     keys_ref,
     partner_ref,
@@ -291,62 +280,50 @@
     query_ref,
 ):
     height, columns = out_ref.shape
-    pixels, _ = own_ref.shape
+    pixels, width = query_ref.shape
     size = 2 * columns
     blocks = pixels // size
     per = slot_ref.shape[0] // blocks
+    sides = left_ref.shape[0]
     start = 2 * columns
+    pad = (halo_ref.shape[0] - start) // 2
+    halo_ref[start:] = jnp.zeros((2 * pad, width), bf16)
     halo_ref[0:columns] = top_ref[...]
     halo_ref[columns:start] = bottom_ref[...]
-    place = start
-    for ref in (left_ref, right_ref, above_left, above_right, below_left, below_right):
-        halo_ref[place : place + ref.shape[0]] = ref[...]
-        place += ref.shape[0]
+    halo_ref[start : start + sides] = left_ref[...]
+    halo_ref[start + pad : start + pad + sides] = right_ref[...]
     carried = jnp.dot(halo_ref[...], prop_ref[...], preferred_element_type=f32)
     high_ref[...], low_ref[...] = split(carried)
+
+    def gap(rows, lanes):
+        mine = lax.broadcasted_iota(jnp.int32, (rows, lanes), 0)
+        return lax.broadcasted_iota(jnp.int32, (rows, lanes), 1) - mine
+
+    along = gap(columns, columns)
+    level = (along >= -1) & (along <= 1)
+    down = gap(height, pad)
+    upright = (down >= 0) & (down <= 2)
+    refs = (halo_ref, high_ref, low_ref)
+    above = outside(first_row[...], *refs, slice(0, columns), level)
+    below = outside(last_row[...], *refs, slice(columns, start), level)
+    before = outside(first_col[...], *refs, slice(start, start + pad), upright)
+    after = outside(last_col[...], *refs, slice(start + pad, start + 2 * pad), upright)
 
     here = lax.broadcasted_iota(jnp.int32, (size, size), 0)
     there = lax.broadcasted_iota(jnp.int32, (size, size), 1)
     mirrored = (here // columns == there // columns) & (
         here % columns + there % columns == columns - 1
     )
-    pix = lax.broadcasted_iota(jnp.int32, (size, columns), 0)
-    oth = lax.broadcasted_iota(jnp.int32, (size, columns), 1)
-    across = oth - pix % columns
-    level = (across >= -1) & (across <= 1)
-    side = place - start
-    spix = lax.broadcasted_iota(jnp.int32, (size, side), 0)
-    soth = lax.broadcasted_iota(jnp.int32, (size, side), 1)
-    far = -4 * pixels
-    srow = jnp.where(soth < height, soth, soth - height)
-    scol = jnp.where(soth < height, -1, columns)
-    lone = soth - 2 * height
-    corners = ((PIECE - 1, -1, -1), (0, -1, columns), (PIECE - 1, height, -1), (0, height, columns))
-    srow = jnp.where(lone >= 0, far, srow)
-    for group, (offset, row, col) in enumerate(corners):
-        here_it_is = lone == group * PIECE + offset
-        srow = jnp.where(here_it_is, row, srow)
-        scol = jnp.where(here_it_is, col, scol)
-    srow = srow - spix // columns
-    scol = scol - spix % columns
-    edge = (scol >= -1) & (scol <= 1)
-
-    for block in range(blocks):
-        at = slice(block * size, (block + 1) * size)
-        own = own_ref[at]
+    column = lax.broadcasted_iota(jnp.int32, (columns, width), 0)
+    for row in range(height):
+        at = slice(row * columns, (row + 1) * columns)
         spread = spread_ref[at]
-        cuts = [(slice(start, place), None)]
-        if block == 0:
-            cuts.append((slice(0, columns), 0))
-        if block == blocks - 1:
-            cuts.append((slice(columns, start), 1))
-        for cut, row in cuts:
-            if row is None:
-                keep = edge & (srow >= 2 * block - 1) & (srow <= 2 * block + 1)
-            else:
-                keep = level & (pix // columns == row)
-            pair = weights(transposed_dot(own, halo_ref[cut]), keep)
-            spread = spread + weighted(pair, high_ref[cut], low_ref[cut])
+        spread = spread + jnp.where(column == 0, before[row : row + 1], 0.0)
+        spread = spread + jnp.where(column == columns - 1, after[row : row + 1], 0.0)
+        if row == 0:
+            spread = spread + above
+        if row == height - 1:
+            spread = spread + below
         query_ref[at] = normalize(spread).astype(bf16)
     for block in range(blocks):
         at = slice(block * size, (block + 1) * size)
@@ -366,28 +343,26 @@
             out_ref[line, :] = mask_ref[line, :].astype(f32) * piece
 
 
-def loss_of(slot, own, spread, halos, w_prop, received, partner, mask):
-    width = own.shape[1]
-    total = sum(halo.shape[0] for halo in halos)
+def loss_of(slot, spread, edges, halos, w_prop, received, partner, mask):
+    columns = mask.shape[1]
+    width = spread.shape[1]
+    pad = -(-halos[2].shape[0] // 16) * 16
+    total = 2 * columns + 2 * pad
     return pl.pallas_call(
         loss_kernel,
-        in_specs=[SMEM] + [VMEM] * 14,
+        in_specs=[SMEM] + [VMEM] * 13,
         out_specs=VMEM,
         out_shape=jax.ShapeDtypeStruct(mask.shape, f32),
-        scratch_shapes=[pltpu.VMEM((total, width), bf16)] * 3 + [pltpu.VMEM(own.shape, bf16)],
+        scratch_shapes=[pltpu.VMEM((total, width), bf16)] * 3 + [pltpu.VMEM(spread.shape, bf16)],
         compiler_params=SMALL,
         name="loss_blocks",
-    )(slot, own, spread, *halos, w_prop, received, partner, mask)
-
-
-def moved(value, down, across):
-    rows, cols = lax.axis_size("rows"), lax.axis_size("cols")
-    pairs = []
-    for row in range(rows):
-        for col in range(cols):
-            if 0 <= row + down < rows and 0 <= col + across < cols:
-                pairs.append((row * cols + col, (row + down) * cols + col + across))
-    return lax.ppermute(value, ("rows", "cols"), pairs)
+    )(slot, spread, *edges, *halos, w_prop, received, partner, mask)
+
+
+def shifted(value, axis):
+    devices = lax.axis_size(axis)
+    up = [(i, i + 1) for i in range(devices - 1)]
+    return lax.ppermute(value[0], axis, up), lax.ppermute(value[1], axis, [(j, i) for i, j in up])
 
 
 def per_device(feat_query, feat_key, w_hidden, w_out, w_prop, valid_mask, neg_shard, neg_block):
@@ -406,20 +381,14 @@
     received = received.reshape(shards * CAP, 128, width)
     feat_query, _ = lax.optimization_barrier((feat_query, send))
     query, *edges = project(feat_query, w_hidden, w_out, True)
-    first_row, last_row, first_col, last_col, *corners = edges
-    steps = (
-        (last_row, 1, 0),
-        (first_row, -1, 0),
-        (last_col, 0, 1),
-        (first_col, 0, -1),
-        (corners[3], 1, 1),
-        (corners[2], 1, -1),
-        (corners[1], -1, 1),
-        (corners[0], -1, -1),
-    )
-    halos = [moved(value, down, across) for value, down, across in steps]
-    spread, own = propagate(query, w_prop, columns)
-    return loss_of(slot, own, spread, halos, w_prop, received, partner, valid_mask)
+    first_row, last_row, first_col, last_col = edges
+    top, bottom = shifted((last_row, first_row), "rows")
+    first = jnp.concatenate([top[:1], first_col, bottom[:1]])
+    last = jnp.concatenate([top[-1:], last_col, bottom[-1:]])
+    left, right = shifted((last, first), "cols")
+    halos = (top, bottom, left, right)
+    spread = propagate(query, w_prop, columns)
+    return loss_of(slot, spread, edges, halos, w_prop, received, partner, valid_mask)
 
 
 def solution(mesh):

time: 96.8 us -> 89 us (0.919)
  the two profiles are of different devices: /device:TPU:27 before, /device:TPU:1 now
where the time goes in v4:
time: 89 us; the launch traced here: 88.3 us
  Pallas kernels  36.8 us (41%)
  starting transfers between devices  32.3 us (36%)
  waiting for transfers between devices  13.6 us (15%)
  local copies, waits for them, and re-layouts  3.96 us (4%)
  other arithmetic  1.42 us (2%)
    pallas_call x2, Pallas kernels, project(): pl.pallas_call(functools.partial(project_kernel, columns=columns), in_spe...  29.3 us
    ppermute x2, waiting for transfers between devices, shifted(): lax.ppermute(value[1], axis, [(j, i) for i, j in up])  13.6 us
    all_to_all x1, starting transfers between devices, per_device(): req = lax.all_to_all(want, 'rows', 0, 0, tiled=True)  9.46 us
    ppermute x2, starting transfers between devices, shifted(): lax.ppermute(value[0], axis, up)  9.45 us
    all_to_all x1, starting transfers between devices, per_device(): received = lax.all_to_all(send, 'rows', 0, 0, tiled=True)  7.24 us
    unnamed x24, local copies, waits for them, and re-layouts  3.94 us
    ppermute x2, starting transfers between devices, shifted(): lax.ppermute(value[1], axis, [(j, i) for i, j in up])  3.44 us
    ppermute x1, starting transfers between devices, per_device(): lax.ppermute(key_map, 'cols', [(i, cols - 1 - i) for i in range(cols)])  2.67 us
  transfers between devices with their start and end apart: 7, of which 2 were waited for; matrix products, arithmetic and copies ran while one was open for 2% of the time, Pallas kernels for 35%

profile of v4, /device:TPU:1, one launch (start us, length us, event | category | flops | bytes accessed | tf_op | source)
XLA Modules:
  0.0 88.3 jit_solution(5827138162048503360)
XLA Ops:
  0.0 1.5 %plan_slots.1 = (s32[16,1,128]{2,1,0:T(1,128)}, s32[16]{0:T(128)}) custom-call(s32[1,1,2,8]{3,2,1,0:T(2,128)} %bitcast.8, s32[1,1,2,8]{3,2,1,0:T(2,128)} %bitcast.9), custom_call_target="tpu_custom_call" | custom-call | tf_op jit(solution)/shard_map/plan_slots/pallas_call | solution.py:64
  1.5 9.5 %all-to-all-start = ((s32[16,1,128]{2,1,0:T(1,128)}), s32[16,1,128]{2,1,0:T(1,128)S(1)}, u32[]{:S(2)}, u32[]{:S(2)}) async-start(s32[16,1,128]{2,1,0:T(1,128)} %get-tuple-element.14), calls=%async_computation | async-start | bytes 16384 | tf_op jit(solution)/shard_map/all_to_all | solution.py:375
  11.0 14.6 %shard_map.82 = bf16[1024,256]{1,0:T(8,128)(2,1)} custom-call(bf16[1024,2048]{1,0:T(8,128)(2,1)} %bitcast.10, bf16[2048,2048]{1,0:T(8,128)(2,1)} %refs_1_.3, bf16[2048,256]{1,0:T(8,128)(2,1)} %refs_2_.3), custom_call_target="tpu_custom_call" | custom-call | flops 9663676416 | bytes 13631488 | tf_op jit(solution)/shard_map/pallas_call | solution.py:148
  25.5 0.0 all-to-all-done.req_ref
  25.5 0.0 copy-start
  25.5 1.0 %copy-done = bf16[1024,256]{1,0:T(8,128)(2,1)S(1)} copy-done((bf16[1024,256]{1,0:T(8,128)(2,1)S(1)}, bf16[1024,256]{1,0:T(8,128)(2,1)}, u32[]{:S(2)}) %copy-start) | copy-done | bytes 524312
  26.6 2.0 %pack_blocks.1 = bf16[16,2,128,256]{3,2,1,0:T(8,128)(2,1)} custom-call(s32[16,1,128]{2,1,0:T(1,128)S(1)} %all-to-all-done.req_ref, bf16[8,128,256]{2,1,0:T(8,128)(2,1)S(1)} %bitcast.7), custom_call_target="tpu_custom_call" | custom-call | tf_op jit(solution)/shard_map/pack_blocks/pallas_call | solution.py:179
  28.6 7.2 %all-to-all-start.1 = ((bf16[16,2,128,256]{3,2,1,0:T(8,128)(2,1)}), bf16[16,2,128,256]{3,2,1,0:T(8,128)(2,1)S(1)}, u32[]{:S(2)}, u32[]{:S(2)}) async-start(bf16[16,2,128,256]{3,2,1,0:T(8,128)(2,1)} %pack_blocks.1), calls=%async_computation.1 | async-start | bytes 4194304 | tf_op jit(solution)/shard_map/all_to_all | solution.py:380
  35.8 0.0 copy-start.4
  35.9 14.7 %shard_map.83 = (bf16[1024,256]{1,0:T(8,128)(2,1)}, bf16[64,256]{1,0:T(8,128)(2,1)}, bf16[64,256]{1,0:T(8,128)(2,1)}, bf16[16,256]{1,0:T(8,128)(2,1)}, bf16[16,256]{1,0:T(8,128)(2,1)}) custom-call(bf16[1024,2048]{1,0:T(8,128)(2,1)} %bitcast.11, bf16[2048,2048]{1,0:T(8,128)(2,1)} %refs_1_.3, bf16[2048,256]{1,0:T(8,128)(2,1)} %refs_2_.3), custom_call_target="tpu_custom_call" | custom-call | flops 9663676416 | bytes 13631488 | tf_op jit(solution)/shard_map/pallas_call | solution.py:148
  50.6 0.0 copy-start.5
  50.6 0.0 copy-start.6
  50.6 0.0 copy-start.7
  50.6 0.0 copy-start.9
  50.6 2.1 %collective-permute-start.1 = (bf16[64,256]{1,0:T(8,128)(2,1)}, bf16[64,256]{1,0:T(8,128)(2,1)S(1)}, u32[]{:S(2)}, u32[]{:S(2)}) collective-permute-start(bf16[64,256]{1,0:T(8,128)(2,1)} %get-tuple-element.17.first_row), channel_id=1, source_target_pairs={{8,0},{16,8},{24,16},{32,24},{40,32},{48,40},{56,48},{64,56},{72,6... | collective-permute-start | bytes 98312 | tf_op jit(solution)/shard_map/ppermute | solution.py:365
  52.8 2.7 %collective-permute-start.4 = (bf16[1024,256]{1,0:T(8,128)(2,1)S(1)}, bf16[1024,256]{1,0:T(8,128)(2,1)S(1)}, u32[]{:S(2)}, u32[]{:S(2)}) collective-permute-start(bf16[1024,256]{1,0:T(8,128)(2,1)S(1)} %copy-done.1), channel_id=1, source_target_pairs={{0,7},{1,6},{2,5},{3,4},{4,3},{5,2},{6,1},{7,0},{8,15},{9,14},{10,... | collective-permute-start | bytes 1572872 | tf_op jit(solution)/shard_map/ppermute | solution.py:378
  55.5 5.9 %collective-permute-start = (bf16[64,256]{1,0:T(8,128)(2,1)}, bf16[64,256]{1,0:T(8,128)(2,1)S(1)}, u32[]{:S(2)}, u32[]{:S(2)}) collective-permute-start(bf16[64,256]{1,0:T(8,128)(2,1)} %get-tuple-element.18.last_row), channel_id=1, source_target_pairs={{0,8},{8,16},{16,24},{24,32},{32,40},{40,48},{48,56},{56,64},{64,7... | collective-permute-start | bytes 98312 | tf_op jit(solution)/shard_map/ppermute | solution.py:365
  61.4 13.2 %collective-permute-done.1.bottom_ref = bf16[64,256]{1,0:T(8,128)(2,1)S(1)} collective-permute-done((bf16[64,256]{1,0:T(8,128)(2,1)}, bf16[64,256]{1,0:T(8,128)(2,1)S(1)}, u32[]{:S(2)}, u32[]{:S(2)}) %collective-permute-start.1) | collective-permute-done | bytes 32800 | tf_op jit(solution)/shard_map/ppermute | solution.py:365
  74.6 0.0 collective-permute-done.top_ref
  74.6 0.7 pad_maximum_fusion
  75.3 3.5 %collective-permute-start.2 = (bf16[18,256]{1,0:T(8,128)(2,1)S(1)}, bf16[18,256]{1,0:T(8,128)(2,1)S(1)}, u32[]{:S(2)}, u32[]{:S(2)}) collective-permute-start(bf16[18,256]{1,0:T(8,128)(2,1)S(1)} %pad_maximum_fusion), channel_id=1, source_target_pairs={{0,1},{1,2},{2,3},{3,4},{4,5},{5,6},{6,7},{8,9},{9,10},{10,11},{11... | collective-permute-start | bytes 27656 | tf_op jit(solution)/shard_map/ppermute | solution.py:365
  78.9 0.7 pad_maximum_fusion.1
  79.6 1.3 %collective-permute-start.3 = (bf16[18,256]{1,0:T(8,128)(2,1)S(1)}, bf16[18,256]{1,0:T(8,128)(2,1)S(1)}, u32[]{:S(2)}, u32[]{:S(2)}) collective-permute-start(bf16[18,256]{1,0:T(8,128)(2,1)S(1)} %pad_maximum_fusion.1), channel_id=1, source_target_pairs={{1,0},{2,1},{3,2},{4,3},{5,4},{6,5},{7,6},{9,8},{10,9},{11,10},{12... | collective-permute-start | bytes 27656 | tf_op jit(solution)/shard_map/ppermute | solution.py:365
  80.9 1.0 %copy-done.11 = bf16[1024,256]{1,0:T(8,128)(2,1)S(1)} copy-done((bf16[1024,256]{1,0:T(8,128)(2,1)S(1)}, bf16[1024,256]{1,0:T(8,128)(2,1)}, u32[]{:S(2)}) %copy-start.11) | copy-done | bytes 524312
  81.9 1.6 %propagate.1.spread_ref = f32[1024,256]{1,0:T(8,128)S(1)} custom-call(bf16[1024,256]{1,0:T(8,128)(2,1)S(1)} %copy-done.11, bf16[256,256]{1,0:T(8,128)(2,1)S(1)} %copy-done.4), custom_call_target="tpu_custom_call" | custom-call | flops 2000000000 | bytes 2000000 | tf_op jit(solution)/shard_map/propagate/pallas_call | solution.py:237
  83.5 0.0 collective-permute-done.2.left_ref
  83.5 0.5 collective-permute-done.3.right_ref
  84.0 0.0 collective-permute-done.4.partner_ref
  84.0 0.8 copy-done.2
  84.8 0.0 all-to-all-done.1
  84.9 1.0 %copy-done.3 = bf16[1024,256]{1,0:T(8,128)(2,1)S(1)} copy-done((bf16[1024,256]{1,0:T(8,128)(2,1)S(1)}, bf16[1024,256]{1,0:T(8,128)(2,1)}, u32[]{:S(2)}) %copy-start.3) | copy-done | bytes 524312
  85.9 2.4 %loss_blocks.1 = f32[16,64]{1,0:T(8,128)} custom-call(s32[16]{0:T(128)S(1)} %copy-done.10, f32[1024,256]{1,0:T(8,128)S(1)} %propagate.1.spread_ref, bf16[64,256]{1,0:T(8,128)(2,1)S(1)} %copy-done.5, bf16[64,256]{1,0:T(8,128)(2,1)S(1)} %copy-done.6, bf16[16,256]{1,0:T(8,128)(2,1)S(1)} %copy-done.7, bf16[16,256]{1,0:T(8,128)(2,1)S(1)} %copy-done.8, ...), custom_call_target="tpu_custom_call" | custom-call | tf_op jit(solution)/shard_map/loss_blocks/pallas_call | solution.py:351
  (16 shorter events, 0.0 us)
Async XLA Ops:
  1.5 24.0 %all-to-all-start = ((s32[16,1,128]{2,1,0:T(1,128)}), s32[16,1,128]{2,1,0:T(1,128)S(1)}, u32[]{:S(2)}, u32[]{:S(2)}) async-start(s32[16,1,128]{2,1,0:T(1,128)} %get-tuple-element.14), calls=%async_computation | async-start | bytes 16384 | tf_op jit(solution)/shard_map/all_to_all | solution.py:375
  25.5 1.0 %copy-start = (bf16[1024,256]{1,0:T(8,128)(2,1)S(1)}, bf16[1024,256]{1,0:T(8,128)(2,1)}, u32[]{:S(2)}) copy-start(bf16[1024,256]{1,0:T(8,128)(2,1)} %shard_map.82) | copy-start | bytes 1572868
  28.6 56.2 %all-to-all-start.1 = ((bf16[16,2,128,256]{3,2,1,0:T(8,128)(2,1)}), bf16[16,2,128,256]{3,2,1,0:T(8,128)(2,1)S(1)}, u32[]{:S(2)}, u32[]{:S(2)}) async-start(bf16[16,2,128,256]{3,2,1,0:T(8,128)(2,1)} %pack_blocks.1), calls=%async_computation.1 | async-start | bytes 4194304 | tf_op jit(solution)/shard_map/all_to_all | solution.py:380
  35.8 17.0 %copy-start.1 = (bf16[1024,256]{1,0:T(8,128)(2,1)S(1)}, bf16[1024,256]{1,0:T(8,128)(2,1)}, u32[]{:S(2)}) copy-start(bf16[1024,256]{1,0:T(8,128)(2,1)} %shard_map.82) | copy-start | bytes 1572868
  35.8 45.0 %copy-start.4 = (bf16[256,256]{1,0:T(8,128)(2,1)S(1)}, bf16[256,256]{1,0:T(8,128)(2,1)}, u32[]{:S(2)}) copy-start(bf16[256,256]{1,0:T(8,128)(2,1)} %prop_ref.3) | copy-start | bytes 393220
  50.6 34.2 %copy-start.5 = (bf16[64,256]{1,0:T(8,128)(2,1)S(1)}, bf16[64,256]{1,0:T(8,128)(2,1)}, u32[]{:S(2)}) copy-start(bf16[64,256]{1,0:T(8,128)(2,1)} %get-tuple-element.17.first_row) | copy-start | bytes 98308
  50.6 34.2 %copy-start.6 = (bf16[64,256]{1,0:T(8,128)(2,1)S(1)}, bf16[64,256]{1,0:T(8,128)(2,1)}, u32[]{:S(2)}) copy-start(bf16[64,256]{1,0:T(8,128)(2,1)} %get-tuple-element.18.last_row) | copy-start | bytes 98308
  50.6 34.2 %copy-start.7 = (bf16[16,256]{1,0:T(8,128)(2,1)S(1)}, bf16[16,256]{1,0:T(8,128)(2,1)}, u32[]{:S(2)}) copy-start(bf16[16,256]{1,0:T(8,128)(2,1)} %get-tuple-element.19.first_col) | copy-start | bytes 24580
  50.6 34.2 %copy-start.8 = (bf16[16,256]{1,0:T(8,128)(2,1)S(1)}, bf16[16,256]{1,0:T(8,128)(2,1)}, u32[]{:S(2)}) copy-start(bf16[16,256]{1,0:T(8,128)(2,1)} %get-tuple-element.20.last_col) | copy-start | bytes 24580
  50.6 34.2 %copy-start.9 = (s32[16,64]{1,0:T(8,128)S(1)}, s32[16,64]{1,0:T(8,128)}, u32[]{:S(2)}) copy-start(s32[16,64]{1,0:T(8,128)} %mask_ref.1) | copy-start | bytes 12292
  50.6 34.2 %copy-start.10 = (s32[16]{0:T(128)S(1)}, s32[16]{0:T(128)}, u32[]{:S(2)}) copy-start(s32[16]{0:T(128)} %get-tuple-element.13.slot_ref) | copy-start | bytes 196
  50.6 23.9 %collective-permute-start.1 = (bf16[64,256]{1,0:T(8,128)(2,1)}, bf16[64,256]{1,0:T(8,128)(2,1)S(1)}, u32[]{:S(2)}, u32[]{:S(2)}) collective-permute-start(bf16[64,256]{1,0:T(8,128)(2,1)} %get-tuple-element.17.first_row), channel_id=1, source_target_pairs={{8,0},{16,8},{24,16},{32,24},{40,32},{48,40},{56,48},{64,56},{72,6... | collective-permute-start | bytes 98312 | tf_op jit(solution)/shard_map/ppermute | solution.py:365
  52.8 31.2 %collective-permute-start.4 = (bf16[1024,256]{1,0:T(8,128)(2,1)S(1)}, bf16[1024,256]{1,0:T(8,128)(2,1)S(1)}, u32[]{:S(2)}, u32[]{:S(2)}) collective-permute-start(bf16[1024,256]{1,0:T(8,128)(2,1)S(1)} %copy-done.1), channel_id=1, source_target_pairs={{0,7},{1,6},{2,5},{3,4},{4,3},{5,2},{6,1},{7,0},{8,15},{9,14},{10,... | collective-permute-start | bytes 1572872 | tf_op jit(solution)/shard_map/ppermute | solution.py:378
  55.5 19.1 %collective-permute-start = (bf16[64,256]{1,0:T(8,128)(2,1)}, bf16[64,256]{1,0:T(8,128)(2,1)S(1)}, u32[]{:S(2)}, u32[]{:S(2)}) collective-permute-start(bf16[64,256]{1,0:T(8,128)(2,1)} %get-tuple-element.18.last_row), channel_id=1, source_target_pairs={{0,8},{8,16},{16,24},{24,32},{32,40},{40,48},{48,56},{56,64},{64,7... | collective-permute-start | bytes 98312 | tf_op jit(solution)/shard_map/ppermute | solution.py:365
  75.3 8.2 %collective-permute-start.2 = (bf16[18,256]{1,0:T(8,128)(2,1)S(1)}, bf16[18,256]{1,0:T(8,128)(2,1)S(1)}, u32[]{:S(2)}, u32[]{:S(2)}) collective-permute-start(bf16[18,256]{1,0:T(8,128)(2,1)S(1)} %pad_maximum_fusion), channel_id=1, source_target_pairs={{0,1},{1,2},{2,3},{3,4},{4,5},{5,6},{6,7},{8,9},{9,10},{10,11},{11... | collective-permute-start | bytes 27656 | tf_op jit(solution)/shard_map/ppermute | solution.py:365
  79.6 4.4 %collective-permute-start.3 = (bf16[18,256]{1,0:T(8,128)(2,1)S(1)}, bf16[18,256]{1,0:T(8,128)(2,1)S(1)}, u32[]{:S(2)}, u32[]{:S(2)}) collective-permute-start(bf16[18,256]{1,0:T(8,128)(2,1)S(1)} %pad_maximum_fusion.1), channel_id=1, source_target_pairs={{1,0},{2,1},{3,2},{4,3},{5,4},{6,5},{7,6},{9,8},{10,9},{11,10},{12... | collective-permute-start | bytes 27656 | tf_op jit(solution)/shard_map/ppermute | solution.py:365
  80.9 1.0 %copy-start.11 = (bf16[1024,256]{1,0:T(8,128)(2,1)S(1)}, bf16[1024,256]{1,0:T(8,128)(2,1)}, u32[]{:S(2)}) copy-start(bf16[1024,256]{1,0:T(8,128)(2,1)} %get-tuple-element.16.own_any) | copy-start | bytes 1572868
  84.0 0.8 copy-start.2
  84.9 1.0 %copy-start.3 = (bf16[1024,256]{1,0:T(8,128)(2,1)S(1)}, bf16[1024,256]{1,0:T(8,128)(2,1)}, u32[]{:S(2)}) copy-start(bf16[1024,256]{1,0:T(8,128)(2,1)} %copy-done.2) | copy-start | bytes 1572868

commit v5 on v4

--- a/solution.py
+++ b/solution.py
@@ -80,6 +80,7 @@
 
 
 PARTS = 4
+FIRST = 4
 
 
 def project_kernel(*refs, columns):
@@ -87,7 +88,7 @@
     edges = refs[4:-5]
     feat, total, hidden_w, out_w, sems = refs[-5:]
     pixels, channels = feat_hbm.shape
-    half = pixels // 2
+    half = pixels // FIRST
     span = channels // PARTS
     cuts = [slice(part * span, (part + 1) * span) for part in range(PARTS)]
 
@@ -152,7 +153,7 @@
         out_shape=[jax.ShapeDtypeStruct((size, width), bf16) for size in sizes],
         scratch_shapes=[
             pltpu.VMEM((pixels, channels), bf16),
-            pltpu.VMEM((pixels // 2, hidden), f32),
+            pltpu.VMEM((pixels // FIRST, hidden), f32),
             pltpu.VMEM((channels, hidden), bf16),
             pltpu.VMEM((hidden, width), bf16),
             pltpu.SemaphoreType.DMA((2 * PARTS + 2,)),

time: 89 us -> 88.4 us (level)
  Pallas kernels: 36.8 us -> 35.6 us
    pallas_call x2, Pallas kernels: 29.3 us -> 28.1 us  [project(): pl.pallas_call(functools.partial(project_kernel, columns=columns), in_spe...]
  transfers between devices with their start and end apart: 7 -> 7, of which waited for: 2 -> 2; matrix products, arithmetic and copies ran while one was open for 2% -> 2% of each run, Pallas kernels for 35% -> 34%
where the time goes in v5:
time: 88.4 us; the launch traced here: 87.7 us
  Pallas kernels  35.6 us (40%)
  starting transfers between devices  32.3 us (37%)
  waiting for transfers between devices  14.2 us (16%)
  local copies, waits for them, and re-layouts  3.96 us (4%)
  other arithmetic  1.42 us (2%)
    pallas_call x2, Pallas kernels, project(): pl.pallas_call(functools.partial(project_kernel, columns=columns), in_spe...  28.1 us
    ppermute x2, waiting for transfers between devices, shifted(): lax.ppermute(value[1], axis, [(j, i) for i, j in up])  14.2 us
    all_to_all x1, starting transfers between devices, per_device(): req = lax.all_to_all(want, 'rows', 0, 0, tiled=True)  9.46 us
    ppermute x2, starting transfers between devices, shifted(): lax.ppermute(value[0], axis, up)  9.44 us
    all_to_all x1, starting transfers between devices, per_device(): received = lax.all_to_all(send, 'rows', 0, 0, tiled=True)  7.24 us
    unnamed x24, local copies, waits for them, and re-layouts  3.94 us
    ppermute x2, starting transfers between devices, shifted(): lax.ppermute(value[1], axis, [(j, i) for i, j in up])  3.44 us
    ppermute x1, starting transfers between devices, per_device(): lax.ppermute(key_map, 'cols', [(i, cols - 1 - i) for i in range(cols)])  2.67 us
  transfers between devices with their start and end apart: 7, of which 2 were waited for; matrix products, arithmetic and copies ran while one was open for 2% of the time, Pallas kernels for 34%

profile of v5, /device:TPU:1, one launch (start us, length us, event | category | flops | bytes accessed | tf_op | source)
XLA Modules:
  0.0 87.7 jit_solution(1625386670716356847)
XLA Ops:
  0.0 1.5 %plan_slots.1 = (s32[16,1,128]{2,1,0:T(1,128)}, s32[16]{0:T(128)}) custom-call(s32[1,1,2,8]{3,2,1,0:T(2,128)} %bitcast.8, s32[1,1,2,8]{3,2,1,0:T(2,128)} %bitcast.9), custom_call_target="tpu_custom_call" | custom-call | tf_op jit(solution)/shard_map/plan_slots/pallas_call | solution.py:64
  1.5 9.5 %all-to-all-start = ((s32[16,1,128]{2,1,0:T(1,128)}), s32[16,1,128]{2,1,0:T(1,128)S(1)}, u32[]{:S(2)}, u32[]{:S(2)}) async-start(s32[16,1,128]{2,1,0:T(1,128)} %get-tuple-element.14), calls=%async_computation | async-start | bytes 16384 | tf_op jit(solution)/shard_map/all_to_all | solution.py:376
  11.0 14.0 %shard_map.82 = bf16[1024,256]{1,0:T(8,128)(2,1)} custom-call(bf16[1024,2048]{1,0:T(8,128)(2,1)} %bitcast.10, bf16[2048,2048]{1,0:T(8,128)(2,1)} %refs_1_.3, bf16[2048,256]{1,0:T(8,128)(2,1)} %refs_2_.3), custom_call_target="tpu_custom_call" | custom-call | flops 9663676416 | bytes 13631488 | tf_op jit(solution)/shard_map/pallas_call | solution.py:149
  25.0 0.0 all-to-all-done.req_ref
  25.0 0.0 copy-start
  25.0 1.0 %copy-done = bf16[1024,256]{1,0:T(8,128)(2,1)S(1)} copy-done((bf16[1024,256]{1,0:T(8,128)(2,1)S(1)}, bf16[1024,256]{1,0:T(8,128)(2,1)}, u32[]{:S(2)}) %copy-start) | copy-done | bytes 524312
  26.0 2.0 %pack_blocks.1 = bf16[16,2,128,256]{3,2,1,0:T(8,128)(2,1)} custom-call(s32[16,1,128]{2,1,0:T(1,128)S(1)} %all-to-all-done.req_ref, bf16[8,128,256]{2,1,0:T(8,128)(2,1)S(1)} %bitcast.7), custom_call_target="tpu_custom_call" | custom-call | tf_op jit(solution)/shard_map/pack_blocks/pallas_call | solution.py:180
  28.0 7.2 %all-to-all-start.1 = ((bf16[16,2,128,256]{3,2,1,0:T(8,128)(2,1)}), bf16[16,2,128,256]{3,2,1,0:T(8,128)(2,1)S(1)}, u32[]{:S(2)}, u32[]{:S(2)}) async-start(bf16[16,2,128,256]{3,2,1,0:T(8,128)(2,1)} %pack_blocks.1), calls=%async_computation.1 | async-start | bytes 4194304 | tf_op jit(solution)/shard_map/all_to_all | solution.py:381
  35.3 0.0 copy-start.4
  35.3 14.1 %shard_map.83 = (bf16[1024,256]{1,0:T(8,128)(2,1)}, bf16[64,256]{1,0:T(8,128)(2,1)}, bf16[64,256]{1,0:T(8,128)(2,1)}, bf16[16,256]{1,0:T(8,128)(2,1)}, bf16[16,256]{1,0:T(8,128)(2,1)}) custom-call(bf16[1024,2048]{1,0:T(8,128)(2,1)} %bitcast.11, bf16[2048,2048]{1,0:T(8,128)(2,1)} %refs_1_.3, bf16[2048,256]{1,0:T(8,128)(2,1)} %refs_2_.3), custom_call_target="tpu_custom_call" | custom-call | flops 9663676416 | bytes 13631488 | tf_op jit(solution)/shard_map/pallas_call | solution.py:149
  49.4 0.0 copy-start.5
  49.5 0.0 copy-start.6
  49.5 0.0 copy-start.7
  49.5 0.0 copy-start.9
  49.5 2.2 %collective-permute-start.1 = (bf16[64,256]{1,0:T(8,128)(2,1)}, bf16[64,256]{1,0:T(8,128)(2,1)S(1)}, u32[]{:S(2)}, u32[]{:S(2)}) collective-permute-start(bf16[64,256]{1,0:T(8,128)(2,1)} %get-tuple-element.17.first_row), channel_id=1, source_target_pairs={{8,0},{16,8},{24,16},{32,24},{40,32},{48,40},{56,48},{64,56},{72,6... | collective-permute-start | bytes 98312 | tf_op jit(solution)/shard_map/ppermute | solution.py:366
  51.7 2.7 %collective-permute-start.4 = (bf16[1024,256]{1,0:T(8,128)(2,1)S(1)}, bf16[1024,256]{1,0:T(8,128)(2,1)S(1)}, u32[]{:S(2)}, u32[]{:S(2)}) collective-permute-start(bf16[1024,256]{1,0:T(8,128)(2,1)S(1)} %copy-done.1), channel_id=1, source_target_pairs={{0,7},{1,6},{2,5},{3,4},{4,3},{5,2},{6,1},{7,0},{8,15},{9,14},{10,... | collective-permute-start | bytes 1572872 | tf_op jit(solution)/shard_map/ppermute | solution.py:379
  54.4 5.9 %collective-permute-start = (bf16[64,256]{1,0:T(8,128)(2,1)}, bf16[64,256]{1,0:T(8,128)(2,1)S(1)}, u32[]{:S(2)}, u32[]{:S(2)}) collective-permute-start(bf16[64,256]{1,0:T(8,128)(2,1)} %get-tuple-element.18.last_row), channel_id=1, source_target_pairs={{0,8},{8,16},{16,24},{24,32},{32,40},{40,48},{48,56},{56,64},{64,7... | collective-permute-start | bytes 98312 | tf_op jit(solution)/shard_map/ppermute | solution.py:366
  60.3 13.7 %collective-permute-done.1.bottom_ref = bf16[64,256]{1,0:T(8,128)(2,1)S(1)} collective-permute-done((bf16[64,256]{1,0:T(8,128)(2,1)}, bf16[64,256]{1,0:T(8,128)(2,1)S(1)}, u32[]{:S(2)}, u32[]{:S(2)}) %collective-permute-start.1) | collective-permute-done | bytes 32800 | tf_op jit(solution)/shard_map/ppermute | solution.py:366
  74.0 0.0 collective-permute-done.top_ref
  74.0 0.7 pad_maximum_fusion
  74.8 3.5 %collective-permute-start.2 = (bf16[18,256]{1,0:T(8,128)(2,1)S(1)}, bf16[18,256]{1,0:T(8,128)(2,1)S(1)}, u32[]{:S(2)}, u32[]{:S(2)}) collective-permute-start(bf16[18,256]{1,0:T(8,128)(2,1)S(1)} %pad_maximum_fusion), channel_id=1, source_target_pairs={{0,1},{1,2},{2,3},{3,4},{4,5},{5,6},{6,7},{8,9},{9,10},{10,11},{11... | collective-permute-start | bytes 27656 | tf_op jit(solution)/shard_map/ppermute | solution.py:366
  78.3 0.7 pad_maximum_fusion.1
  79.0 1.3 %collective-permute-start.3 = (bf16[18,256]{1,0:T(8,128)(2,1)S(1)}, bf16[18,256]{1,0:T(8,128)(2,1)S(1)}, u32[]{:S(2)}, u32[]{:S(2)}) collective-permute-start(bf16[18,256]{1,0:T(8,128)(2,1)S(1)} %pad_maximum_fusion.1), channel_id=1, source_target_pairs={{1,0},{2,1},{3,2},{4,3},{5,4},{6,5},{7,6},{9,8},{10,9},{11,10},{12... | collective-permute-start | bytes 27656 | tf_op jit(solution)/shard_map/ppermute | solution.py:366
  80.3 1.0 %copy-done.11 = bf16[1024,256]{1,0:T(8,128)(2,1)S(1)} copy-done((bf16[1024,256]{1,0:T(8,128)(2,1)S(1)}, bf16[1024,256]{1,0:T(8,128)(2,1)}, u32[]{:S(2)}) %copy-start.11) | copy-done | bytes 524312
  81.4 1.6 %propagate.1.spread_ref = f32[1024,256]{1,0:T(8,128)S(1)} custom-call(bf16[1024,256]{1,0:T(8,128)(2,1)S(1)} %copy-done.11, bf16[256,256]{1,0:T(8,128)(2,1)S(1)} %copy-done.4), custom_call_target="tpu_custom_call" | custom-call | flops 2000000000 | bytes 2000000 | tf_op jit(solution)/shard_map/propagate/pallas_call | solution.py:238
  83.0 0.0 collective-permute-done.2.left_ref
  83.0 0.5 collective-permute-done.3.right_ref
  83.4 0.0 collective-permute-done.4.partner_ref
  83.4 0.8 copy-done.2
  84.2 0.0 all-to-all-done.1
  84.3 1.0 %copy-done.3 = bf16[1024,256]{1,0:T(8,128)(2,1)S(1)} copy-done((bf16[1024,256]{1,0:T(8,128)(2,1)S(1)}, bf16[1024,256]{1,0:T(8,128)(2,1)}, u32[]{:S(2)}) %copy-start.3) | copy-done | bytes 524312
  85.3 2.4 %loss_blocks.1 = f32[16,64]{1,0:T(8,128)} custom-call(s32[16]{0:T(128)S(1)} %copy-done.10, f32[1024,256]{1,0:T(8,128)S(1)} %propagate.1.spread_ref, bf16[64,256]{1,0:T(8,128)(2,1)S(1)} %copy-done.5, bf16[64,256]{1,0:T(8,128)(2,1)S(1)} %copy-done.6, bf16[16,256]{1,0:T(8,128)(2,1)S(1)} %copy-done.7, bf16[16,256]{1,0:T(8,128)(2,1)S(1)} %copy-done.8, ...), custom_call_target="tpu_custom_call" | custom-call | tf_op jit(solution)/shard_map/loss_blocks/pallas_call | solution.py:352
  (16 shorter events, 0.0 us)
Async XLA Ops:
  1.5 23.5 %all-to-all-start = ((s32[16,1,128]{2,1,0:T(1,128)}), s32[16,1,128]{2,1,0:T(1,128)S(1)}, u32[]{:S(2)}, u32[]{:S(2)}) async-start(s32[16,1,128]{2,1,0:T(1,128)} %get-tuple-element.14), calls=%async_computation | async-start | bytes 16384 | tf_op jit(solution)/shard_map/all_to_all | solution.py:376
  25.0 1.0 %copy-start = (bf16[1024,256]{1,0:T(8,128)(2,1)S(1)}, bf16[1024,256]{1,0:T(8,128)(2,1)}, u32[]{:S(2)}) copy-start(bf16[1024,256]{1,0:T(8,128)(2,1)} %shard_map.82) | copy-start | bytes 1572868
  28.0 56.2 %all-to-all-start.1 = ((bf16[16,2,128,256]{3,2,1,0:T(8,128)(2,1)}), bf16[16,2,128,256]{3,2,1,0:T(8,128)(2,1)S(1)}, u32[]{:S(2)}, u32[]{:S(2)}) async-start(bf16[16,2,128,256]{3,2,1,0:T(8,128)(2,1)} %pack_blocks.1), calls=%async_computation.1 | async-start | bytes 4194304 | tf_op jit(solution)/shard_map/all_to_all | solution.py:381
  35.3 16.4 %copy-start.1 = (bf16[1024,256]{1,0:T(8,128)(2,1)S(1)}, bf16[1024,256]{1,0:T(8,128)(2,1)}, u32[]{:S(2)}) copy-start(bf16[1024,256]{1,0:T(8,128)(2,1)} %shard_map.82) | copy-start | bytes 1572868
  35.3 45.0 %copy-start.4 = (bf16[256,256]{1,0:T(8,128)(2,1)S(1)}, bf16[256,256]{1,0:T(8,128)(2,1)}, u32[]{:S(2)}) copy-start(bf16[256,256]{1,0:T(8,128)(2,1)} %prop_ref.3) | copy-start | bytes 393220
  49.4 34.8 %copy-start.5 = (bf16[64,256]{1,0:T(8,128)(2,1)S(1)}, bf16[64,256]{1,0:T(8,128)(2,1)}, u32[]{:S(2)}) copy-start(bf16[64,256]{1,0:T(8,128)(2,1)} %get-tuple-element.17.first_row) | copy-start | bytes 98308
  49.5 34.8 %copy-start.6 = (bf16[64,256]{1,0:T(8,128)(2,1)S(1)}, bf16[64,256]{1,0:T(8,128)(2,1)}, u32[]{:S(2)}) copy-start(bf16[64,256]{1,0:T(8,128)(2,1)} %get-tuple-element.18.last_row) | copy-start | bytes 98308
  49.5 34.8 %copy-start.7 = (bf16[16,256]{1,0:T(8,128)(2,1)S(1)}, bf16[16,256]{1,0:T(8,128)(2,1)}, u32[]{:S(2)}) copy-start(bf16[16,256]{1,0:T(8,128)(2,1)} %get-tuple-element.19.first_col) | copy-start | bytes 24580
  49.5 34.8 %copy-start.8 = (bf16[16,256]{1,0:T(8,128)(2,1)S(1)}, bf16[16,256]{1,0:T(8,128)(2,1)}, u32[]{:S(2)}) copy-start(bf16[16,256]{1,0:T(8,128)(2,1)} %get-tuple-element.20.last_col) | copy-start | bytes 24580
  49.5 34.8 %copy-start.9 = (s32[16,64]{1,0:T(8,128)S(1)}, s32[16,64]{1,0:T(8,128)}, u32[]{:S(2)}) copy-start(s32[16,64]{1,0:T(8,128)} %mask_ref.1) | copy-start | bytes 12292
  49.5 34.8 %copy-start.10 = (s32[16]{0:T(128)S(1)}, s32[16]{0:T(128)}, u32[]{:S(2)}) copy-start(s32[16]{0:T(128)} %get-tuple-element.13.slot_ref) | copy-start | bytes 196
  49.5 24.5 %collective-permute-start.1 = (bf16[64,256]{1,0:T(8,128)(2,1)}, bf16[64,256]{1,0:T(8,128)(2,1)S(1)}, u32[]{:S(2)}, u32[]{:S(2)}) collective-permute-start(bf16[64,256]{1,0:T(8,128)(2,1)} %get-tuple-element.17.first_row), channel_id=1, source_target_pairs={{8,0},{16,8},{24,16},{32,24},{40,32},{48,40},{56,48},{64,56},{72,6... | collective-permute-start | bytes 98312 | tf_op jit(solution)/shard_map/ppermute | solution.py:366
  51.7 31.8 %collective-permute-start.4 = (bf16[1024,256]{1,0:T(8,128)(2,1)S(1)}, bf16[1024,256]{1,0:T(8,128)(2,1)S(1)}, u32[]{:S(2)}, u32[]{:S(2)}) collective-permute-start(bf16[1024,256]{1,0:T(8,128)(2,1)S(1)} %copy-done.1), channel_id=1, source_target_pairs={{0,7},{1,6},{2,5},{3,4},{4,3},{5,2},{6,1},{7,0},{8,15},{9,14},{10,... | collective-permute-start | bytes 1572872 | tf_op jit(solution)/shard_map/ppermute | solution.py:379
  54.4 19.7 %collective-permute-start = (bf16[64,256]{1,0:T(8,128)(2,1)}, bf16[64,256]{1,0:T(8,128)(2,1)S(1)}, u32[]{:S(2)}, u32[]{:S(2)}) collective-permute-start(bf16[64,256]{1,0:T(8,128)(2,1)} %get-tuple-element.18.last_row), channel_id=1, source_target_pairs={{0,8},{8,16},{16,24},{24,32},{32,40},{40,48},{48,56},{56,64},{64,7... | collective-permute-start | bytes 98312 | tf_op jit(solution)/shard_map/ppermute | solution.py:366
  74.8 8.2 %collective-permute-start.2 = (bf16[18,256]{1,0:T(8,128)(2,1)S(1)}, bf16[18,256]{1,0:T(8,128)(2,1)S(1)}, u32[]{:S(2)}, u32[]{:S(2)}) collective-permute-start(bf16[18,256]{1,0:T(8,128)(2,1)S(1)} %pad_maximum_fusion), channel_id=1, source_target_pairs={{0,1},{1,2},{2,3},{3,4},{4,5},{5,6},{6,7},{8,9},{9,10},{10,11},{11... | collective-permute-start | bytes 27656 | tf_op jit(solution)/shard_map/ppermute | solution.py:366
  79.0 4.4 %collective-permute-start.3 = (bf16[18,256]{1,0:T(8,128)(2,1)S(1)}, bf16[18,256]{1,0:T(8,128)(2,1)S(1)}, u32[]{:S(2)}, u32[]{:S(2)}) collective-permute-start(bf16[18,256]{1,0:T(8,128)(2,1)S(1)} %pad_maximum_fusion.1), channel_id=1, source_target_pairs={{1,0},{2,1},{3,2},{4,3},{5,4},{6,5},{7,6},{9,8},{10,9},{11,10},{12... | collective-permute-start | bytes 27656 | tf_op jit(solution)/shard_map/ppermute | solution.py:366
  80.3 1.0 %copy-start.11 = (bf16[1024,256]{1,0:T(8,128)(2,1)S(1)}, bf16[1024,256]{1,0:T(8,128)(2,1)}, u32[]{:S(2)}) copy-start(bf16[1024,256]{1,0:T(8,128)(2,1)} %get-tuple-element.16.own_any) | copy-start | bytes 1572868
  83.4 0.8 copy-start.2
  84.3 1.0 %copy-start.3 = (bf16[1024,256]{1,0:T(8,128)(2,1)S(1)}, bf16[1024,256]{1,0:T(8,128)(2,1)}, u32[]{:S(2)}) copy-start(bf16[1024,256]{1,0:T(8,128)(2,1)} %copy-done.2) | copy-start | bytes 1572868

commit v6 on v5

--- a/solution.py
+++ b/solution.py
@@ -97,10 +97,10 @@
 
     feats = [copy(feat_hbm.at[0:half, c], feat.at[0:half, c], i) for i, c in enumerate(cuts)]
     pieces = [copy(hidden_hbm.at[c], hidden_w.at[c], PARTS + i) for i, c in enumerate(cuts)]
-    later = [
-        copy(out_hbm, out_w, 2 * PARTS),
-        copy(feat_hbm.at[half:pixels], feat.at[half:pixels], 2 * PARTS + 1),
-    ]
+    bounds = (half, pixels // 2, pixels)
+    spans = [slice(low, high) for low, high in zip(bounds, bounds[1:])]
+    later = [copy(out_hbm, out_w, 2 * PARTS)]
+    later += [copy(feat_hbm.at[c], feat.at[c], 2 * PARTS + 1 + i) for i, c in enumerate(spans)]
     for first, second in zip(feats, pieces):
         first.start()
         second.start()
@@ -119,11 +119,12 @@
     later[0].wait()
     raw = jnp.dot(hidden, out_w[...], preferred_element_type=f32)
     map_ref[0:half] = normalize(raw).astype(bf16)
-    later[1].wait()
-    hidden = jnp.dot(feat[half:], hidden_w[...], preferred_element_type=f32)
-    hidden = jnp.maximum(hidden, 0.0).astype(bf16)
-    raw = jnp.dot(hidden, out_w[...], preferred_element_type=f32)
-    map_ref[half:pixels] = normalize(raw).astype(bf16)
+    for load, cut in zip(later[1:], spans):
+        load.wait()
+        hidden = jnp.dot(feat[cut], hidden_w[...], preferred_element_type=f32)
+        hidden = jnp.maximum(hidden, 0.0).astype(bf16)
+        raw = jnp.dot(hidden, out_w[...], preferred_element_type=f32)
+        map_ref[cut] = normalize(raw).astype(bf16)
     if edges:
         first_row, last_row, first_col, last_col = edges
         height = first_col.shape[0]
@@ -156,7 +157,7 @@
             pltpu.VMEM((pixels // FIRST, hidden), f32),
             pltpu.VMEM((channels, hidden), bf16),
             pltpu.VMEM((hidden, width), bf16),
-            pltpu.SemaphoreType.DMA((2 * PARTS + 2,)),
+            pltpu.SemaphoreType.DMA((2 * PARTS + 3,)),
         ],
         compiler_params=pltpu.CompilerParams(vmem_limit_bytes=LIMIT),
         cost_estimate=pl.CostEstimate(

time: 88.4 us -> 88.8 us (level)
  no operation moved by 1% of the time
where the time goes in v6:
time: 88.8 us; the launch traced here: 88.1 us
  Pallas kernels  36.3 us (41%)
  starting transfers between devices  32.3 us (36%)
  waiting for transfers between devices  14 us (16%)
  local copies, waits for them, and re-layouts  3.96 us (4%)
  other arithmetic  1.42 us (2%)
    pallas_call x2, Pallas kernels, project(): pl.pallas_call(functools.partial(project_kernel, columns=columns), in_spe...  28.8 us
    ppermute x2, waiting for transfers between devices, shifted(): lax.ppermute(value[1], axis, [(j, i) for i, j in up])  13.9 us
    all_to_all x1, starting transfers between devices, per_device(): req = lax.all_to_all(want, 'rows', 0, 0, tiled=True)  9.46 us
    ppermute x2, starting transfers between devices, shifted(): lax.ppermute(value[0], axis, up)  9.44 us
    all_to_all x1, starting transfers between devices, per_device(): received = lax.all_to_all(send, 'rows', 0, 0, tiled=True)  7.24 us
    unnamed x24, local copies, waits for them, and re-layouts  3.94 us
    ppermute x2, starting transfers between devices, shifted(): lax.ppermute(value[1], axis, [(j, i) for i, j in up])  3.45 us
    ppermute x1, starting transfers between devices, per_device(): lax.ppermute(key_map, 'cols', [(i, cols - 1 - i) for i in range(cols)])  2.66 us
  transfers between devices with their start and end apart: 7, of which 2 were waited for; matrix products, arithmetic and copies ran while one was open for 2% of the time, Pallas kernels for 34%

profile of v6, /device:TPU:1, one launch (start us, length us, event | category | flops | bytes accessed | tf_op | source)
XLA Modules:
  0.0 88.1 jit_solution(12551876921920153109)
XLA Ops:
  0.0 1.5 %plan_slots.1 = (s32[16,1,128]{2,1,0:T(1,128)}, s32[16]{0:T(128)}) custom-call(s32[1,1,2,8]{3,2,1,0:T(2,128)} %bitcast.8, s32[1,1,2,8]{3,2,1,0:T(2,128)} %bitcast.9), custom_call_target="tpu_custom_call" | custom-call | tf_op jit(solution)/shard_map/plan_slots/pallas_call | solution.py:64
  1.5 9.5 %all-to-all-start = ((s32[16,1,128]{2,1,0:T(1,128)}), s32[16,1,128]{2,1,0:T(1,128)S(1)}, u32[]{:S(2)}, u32[]{:S(2)}) async-start(s32[16,1,128]{2,1,0:T(1,128)} %get-tuple-element.14), calls=%async_computation | async-start | bytes 16384 | tf_op jit(solution)/shard_map/all_to_all | solution.py:377
  11.0 14.4 %shard_map.82 = bf16[1024,256]{1,0:T(8,128)(2,1)} custom-call(bf16[1024,2048]{1,0:T(8,128)(2,1)} %bitcast.10, bf16[2048,2048]{1,0:T(8,128)(2,1)} %refs_1_.3, bf16[2048,256]{1,0:T(8,128)(2,1)} %refs_2_.3), custom_call_target="tpu_custom_call" | custom-call | flops 9663676416 | bytes 13631488 | tf_op jit(solution)/shard_map/pallas_call | solution.py:150
  25.3 0.0 all-to-all-done.req_ref
  25.4 1.0 %copy-done = bf16[1024,256]{1,0:T(8,128)(2,1)S(1)} copy-done((bf16[1024,256]{1,0:T(8,128)(2,1)S(1)}, bf16[1024,256]{1,0:T(8,128)(2,1)}, u32[]{:S(2)}) %copy-start) | copy-done | bytes 524312
  26.4 2.0 %pack_blocks.1 = bf16[16,2,128,256]{3,2,1,0:T(8,128)(2,1)} custom-call(s32[16,1,128]{2,1,0:T(1,128)S(1)} %all-to-all-done.req_ref, bf16[8,128,256]{2,1,0:T(8,128)(2,1)S(1)} %bitcast.7), custom_call_target="tpu_custom_call" | custom-call | tf_op jit(solution)/shard_map/pack_blocks/pallas_call | solution.py:181
  28.4 7.2 %all-to-all-start.1 = ((bf16[16,2,128,256]{3,2,1,0:T(8,128)(2,1)}), bf16[16,2,128,256]{3,2,1,0:T(8,128)(2,1)S(1)}, u32[]{:S(2)}, u32[]{:S(2)}) async-start(bf16[16,2,128,256]{3,2,1,0:T(8,128)(2,1)} %pack_blocks.1), calls=%async_computation.1 | async-start | bytes 4194304 | tf_op jit(solution)/shard_map/all_to_all | solution.py:382
  35.7 0.0 copy-start.4
  35.7 14.4 %shard_map.83 = (bf16[1024,256]{1,0:T(8,128)(2,1)}, bf16[64,256]{1,0:T(8,128)(2,1)}, bf16[64,256]{1,0:T(8,128)(2,1)}, bf16[16,256]{1,0:T(8,128)(2,1)}, bf16[16,256]{1,0:T(8,128)(2,1)}) custom-call(bf16[1024,2048]{1,0:T(8,128)(2,1)} %bitcast.11, bf16[2048,2048]{1,0:T(8,128)(2,1)} %refs_1_.3, bf16[2048,256]{1,0:T(8,128)(2,1)} %refs_2_.3), custom_call_target="tpu_custom_call" | custom-call | flops 9663676416 | bytes 13631488 | tf_op jit(solution)/shard_map/pallas_call | solution.py:150
  50.1 0.0 copy-start.7
  50.1 0.0 copy-start.9
  50.2 2.2 %collective-permute-start.1 = (bf16[64,256]{1,0:T(8,128)(2,1)}, bf16[64,256]{1,0:T(8,128)(2,1)S(1)}, u32[]{:S(2)}, u32[]{:S(2)}) collective-permute-start(bf16[64,256]{1,0:T(8,128)(2,1)} %get-tuple-element.17.first_row), channel_id=1, source_target_pairs={{8,0},{16,8},{24,16},{32,24},{40,32},{48,40},{56,48},{64,56},{72,6... | collective-permute-start | bytes 98312 | tf_op jit(solution)/shard_map/ppermute | solution.py:367
  52.3 2.7 %collective-permute-start.4 = (bf16[1024,256]{1,0:T(8,128)(2,1)S(1)}, bf16[1024,256]{1,0:T(8,128)(2,1)S(1)}, u32[]{:S(2)}, u32[]{:S(2)}) collective-permute-start(bf16[1024,256]{1,0:T(8,128)(2,1)S(1)} %copy-done.1), channel_id=1, source_target_pairs={{0,7},{1,6},{2,5},{3,4},{4,3},{5,2},{6,1},{7,0},{8,15},{9,14},{10,... | collective-permute-start | bytes 1572872 | tf_op jit(solution)/shard_map/ppermute | solution.py:380
  55.0 5.9 %collective-permute-start = (bf16[64,256]{1,0:T(8,128)(2,1)}, bf16[64,256]{1,0:T(8,128)(2,1)S(1)}, u32[]{:S(2)}, u32[]{:S(2)}) collective-permute-start(bf16[64,256]{1,0:T(8,128)(2,1)} %get-tuple-element.18.last_row), channel_id=1, source_target_pairs={{0,8},{8,16},{16,24},{24,32},{32,40},{40,48},{48,56},{56,64},{64,7... | collective-permute-start | bytes 98312 | tf_op jit(solution)/shard_map/ppermute | solution.py:367
  60.9 13.5 %collective-permute-done.1.bottom_ref = bf16[64,256]{1,0:T(8,128)(2,1)S(1)} collective-permute-done((bf16[64,256]{1,0:T(8,128)(2,1)}, bf16[64,256]{1,0:T(8,128)(2,1)S(1)}, u32[]{:S(2)}, u32[]{:S(2)}) %collective-permute-start.1) | collective-permute-done | bytes 32800 | tf_op jit(solution)/shard_map/ppermute | solution.py:367
  74.4 0.0 collective-permute-done.top_ref
  74.4 0.7 pad_maximum_fusion
  75.1 3.5 %collective-permute-start.2 = (bf16[18,256]{1,0:T(8,128)(2,1)S(1)}, bf16[18,256]{1,0:T(8,128)(2,1)S(1)}, u32[]{:S(2)}, u32[]{:S(2)}) collective-permute-start(bf16[18,256]{1,0:T(8,128)(2,1)S(1)} %pad_maximum_fusion), channel_id=1, source_target_pairs={{0,1},{1,2},{2,3},{3,4},{4,5},{5,6},{6,7},{8,9},{9,10},{10,11},{11... | collective-permute-start | bytes 27656 | tf_op jit(solution)/shard_map/ppermute | solution.py:367
  78.7 0.7 pad_maximum_fusion.1
  79.4 1.3 %collective-permute-start.3 = (bf16[18,256]{1,0:T(8,128)(2,1)S(1)}, bf16[18,256]{1,0:T(8,128)(2,1)S(1)}, u32[]{:S(2)}, u32[]{:S(2)}) collective-permute-start(bf16[18,256]{1,0:T(8,128)(2,1)S(1)} %pad_maximum_fusion.1), channel_id=1, source_target_pairs={{1,0},{2,1},{3,2},{4,3},{5,4},{6,5},{7,6},{9,8},{10,9},{11,10},{12... | collective-permute-start | bytes 27656 | tf_op jit(solution)/shard_map/ppermute | solution.py:367
  80.7 1.0 %copy-done.11 = bf16[1024,256]{1,0:T(8,128)(2,1)S(1)} copy-done((bf16[1024,256]{1,0:T(8,128)(2,1)S(1)}, bf16[1024,256]{1,0:T(8,128)(2,1)}, u32[]{:S(2)}) %copy-start.11) | copy-done | bytes 524312
  81.7 1.6 %propagate.1.spread_ref = f32[1024,256]{1,0:T(8,128)S(1)} custom-call(bf16[1024,256]{1,0:T(8,128)(2,1)S(1)} %copy-done.11, bf16[256,256]{1,0:T(8,128)(2,1)S(1)} %copy-done.4), custom_call_target="tpu_custom_call" | custom-call | flops 2000000000 | bytes 2000000 | tf_op jit(solution)/shard_map/propagate/pallas_call | solution.py:239
  83.4 0.0 collective-permute-done.2.left_ref
  83.4 0.5 collective-permute-done.3.right_ref
  83.8 0.0 collective-permute-done.4.partner_ref
  83.8 0.8 copy-done.2
  84.6 0.0 all-to-all-done.1
  84.6 0.0 copy-done.7
  84.7 0.0 copy-done.8
  84.7 0.0 copy-done.9
  84.7 1.0 %copy-done.3 = bf16[1024,256]{1,0:T(8,128)(2,1)S(1)} copy-done((bf16[1024,256]{1,0:T(8,128)(2,1)S(1)}, bf16[1024,256]{1,0:T(8,128)(2,1)}, u32[]{:S(2)}) %copy-start.3) | copy-done | bytes 524312
  85.7 2.4 %loss_blocks.1 = f32[16,64]{1,0:T(8,128)} custom-call(s32[16]{0:T(128)S(1)} %copy-done.10, f32[1024,256]{1,0:T(8,128)S(1)} %propagate.1.spread_ref, bf16[64,256]{1,0:T(8,128)(2,1)S(1)} %copy-done.5, bf16[64,256]{1,0:T(8,128)(2,1)S(1)} %copy-done.6, bf16[16,256]{1,0:T(8,128)(2,1)S(1)} %copy-done.7, bf16[16,256]{1,0:T(8,128)(2,1)S(1)} %copy-done.8, ...), custom_call_target="tpu_custom_call" | custom-call | tf_op jit(solution)/shard_map/loss_blocks/pallas_call | solution.py:353
  (16 shorter events, 0.0 us)
Async XLA Ops:
  1.5 23.9 %all-to-all-start = ((s32[16,1,128]{2,1,0:T(1,128)}), s32[16,1,128]{2,1,0:T(1,128)S(1)}, u32[]{:S(2)}, u32[]{:S(2)}) async-start(s32[16,1,128]{2,1,0:T(1,128)} %get-tuple-element.14), calls=%async_computation | async-start | bytes 16384 | tf_op jit(solution)/shard_map/all_to_all | solution.py:377
  25.4 1.0 %copy-start = (bf16[1024,256]{1,0:T(8,128)(2,1)S(1)}, bf16[1024,256]{1,0:T(8,128)(2,1)}, u32[]{:S(2)}) copy-start(bf16[1024,256]{1,0:T(8,128)(2,1)} %shard_map.82) | copy-start | bytes 1572868
  28.4 56.2 %all-to-all-start.1 = ((bf16[16,2,128,256]{3,2,1,0:T(8,128)(2,1)}), bf16[16,2,128,256]{3,2,1,0:T(8,128)(2,1)S(1)}, u32[]{:S(2)}, u32[]{:S(2)}) async-start(bf16[16,2,128,256]{3,2,1,0:T(8,128)(2,1)} %pack_blocks.1), calls=%async_computation.1 | async-start | bytes 4194304 | tf_op jit(solution)/shard_map/all_to_all | solution.py:382
  35.7 16.7 %copy-start.1 = (bf16[1024,256]{1,0:T(8,128)(2,1)S(1)}, bf16[1024,256]{1,0:T(8,128)(2,1)}, u32[]{:S(2)}) copy-start(bf16[1024,256]{1,0:T(8,128)(2,1)} %shard_map.82) | copy-start | bytes 1572868
  35.7 45.0 %copy-start.4 = (bf16[256,256]{1,0:T(8,128)(2,1)S(1)}, bf16[256,256]{1,0:T(8,128)(2,1)}, u32[]{:S(2)}) copy-start(bf16[256,256]{1,0:T(8,128)(2,1)} %prop_ref.3) | copy-start | bytes 393220
  50.1 34.5 %copy-start.5 = (bf16[64,256]{1,0:T(8,128)(2,1)S(1)}, bf16[64,256]{1,0:T(8,128)(2,1)}, u32[]{:S(2)}) copy-start(bf16[64,256]{1,0:T(8,128)(2,1)} %get-tuple-element.17.first_row) | copy-start | bytes 98308
  50.1 34.5 %copy-start.6 = (bf16[64,256]{1,0:T(8,128)(2,1)S(1)}, bf16[64,256]{1,0:T(8,128)(2,1)}, u32[]{:S(2)}) copy-start(bf16[64,256]{1,0:T(8,128)(2,1)} %get-tuple-element.18.last_row) | copy-start | bytes 98308
  50.1 34.5 %copy-start.7 = (bf16[16,256]{1,0:T(8,128)(2,1)S(1)}, bf16[16,256]{1,0:T(8,128)(2,1)}, u32[]{:S(2)}) copy-start(bf16[16,256]{1,0:T(8,128)(2,1)} %get-tuple-element.19.first_col) | copy-start | bytes 24580
  50.1 34.5 %copy-start.8 = (bf16[16,256]{1,0:T(8,128)(2,1)S(1)}, bf16[16,256]{1,0:T(8,128)(2,1)}, u32[]{:S(2)}) copy-start(bf16[16,256]{1,0:T(8,128)(2,1)} %get-tuple-element.20.last_col) | copy-start | bytes 24580
  50.1 34.5 %copy-start.9 = (s32[16,64]{1,0:T(8,128)S(1)}, s32[16,64]{1,0:T(8,128)}, u32[]{:S(2)}) copy-start(s32[16,64]{1,0:T(8,128)} %mask_ref.1) | copy-start | bytes 12292
  50.1 34.5 %copy-start.10 = (s32[16]{0:T(128)S(1)}, s32[16]{0:T(128)}, u32[]{:S(2)}) copy-start(s32[16]{0:T(128)} %get-tuple-element.13.slot_ref) | copy-start | bytes 196
  50.2 24.3 %collective-permute-start.1 = (bf16[64,256]{1,0:T(8,128)(2,1)}, bf16[64,256]{1,0:T(8,128)(2,1)S(1)}, u32[]{:S(2)}, u32[]{:S(2)}) collective-permute-start(bf16[64,256]{1,0:T(8,128)(2,1)} %get-tuple-element.17.first_row), channel_id=1, source_target_pairs={{8,0},{16,8},{24,16},{32,24},{40,32},{48,40},{56,48},{64,56},{72,6... | collective-permute-start | bytes 98312 | tf_op jit(solution)/shard_map/ppermute | solution.py:367
  52.3 31.5 %collective-permute-start.4 = (bf16[1024,256]{1,0:T(8,128)(2,1)S(1)}, bf16[1024,256]{1,0:T(8,128)(2,1)S(1)}, u32[]{:S(2)}, u32[]{:S(2)}) collective-permute-start(bf16[1024,256]{1,0:T(8,128)(2,1)S(1)} %copy-done.1), channel_id=1, source_target_pairs={{0,7},{1,6},{2,5},{3,4},{4,3},{5,2},{6,1},{7,0},{8,15},{9,14},{10,... | collective-permute-start | bytes 1572872 | tf_op jit(solution)/shard_map/ppermute | solution.py:380
  55.0 19.4 %collective-permute-start = (bf16[64,256]{1,0:T(8,128)(2,1)}, bf16[64,256]{1,0:T(8,128)(2,1)S(1)}, u32[]{:S(2)}, u32[]{:S(2)}) collective-permute-start(bf16[64,256]{1,0:T(8,128)(2,1)} %get-tuple-element.18.last_row), channel_id=1, source_target_pairs={{0,8},{8,16},{16,24},{24,32},{32,40},{40,48},{48,56},{56,64},{64,7... | collective-permute-start | bytes 98312 | tf_op jit(solution)/shard_map/ppermute | solution.py:367
  75.1 8.2 %collective-permute-start.2 = (bf16[18,256]{1,0:T(8,128)(2,1)S(1)}, bf16[18,256]{1,0:T(8,128)(2,1)S(1)}, u32[]{:S(2)}, u32[]{:S(2)}) collective-permute-start(bf16[18,256]{1,0:T(8,128)(2,1)S(1)} %pad_maximum_fusion), channel_id=1, source_target_pairs={{0,1},{1,2},{2,3},{3,4},{4,5},{5,6},{6,7},{8,9},{9,10},{10,11},{11... | collective-permute-start | bytes 27656 | tf_op jit(solution)/shard_map/ppermute | solution.py:367
  79.4 4.4 %collective-permute-start.3 = (bf16[18,256]{1,0:T(8,128)(2,1)S(1)}, bf16[18,256]{1,0:T(8,128)(2,1)S(1)}, u32[]{:S(2)}, u32[]{:S(2)}) collective-permute-start(bf16[18,256]{1,0:T(8,128)(2,1)S(1)} %pad_maximum_fusion.1), channel_id=1, source_target_pairs={{1,0},{2,1},{3,2},{4,3},{5,4},{6,5},{7,6},{9,8},{10,9},{11,10},{12... | collective-permute-start | bytes 27656 | tf_op jit(solution)/shard_map/ppermute | solution.py:367
  80.7 1.0 %copy-start.11 = (bf16[1024,256]{1,0:T(8,128)(2,1)S(1)}, bf16[1024,256]{1,0:T(8,128)(2,1)}, u32[]{:S(2)}) copy-start(bf16[1024,256]{1,0:T(8,128)(2,1)} %get-tuple-element.16.own_any) | copy-start | bytes 1572868
  83.8 0.8 copy-start.2
  84.7 1.0 %copy-start.3 = (bf16[1024,256]{1,0:T(8,128)(2,1)S(1)}, bf16[1024,256]{1,0:T(8,128)(2,1)}, u32[]{:S(2)}) copy-start(bf16[1024,256]{1,0:T(8,128)(2,1)} %copy-done.2) | copy-start | bytes 1572868
